TPU v7x, 128 devices: a whole 4x4x4 slice. The times are simulated.
128 devices in a mesh: seq: 16 (over y, x_lo, core), head: 8 (over x_hi, z).
Axes of the slice: x: 4 (x_hi: 2, x_lo: 2; x = x_hi * 2 + x_lo), y: 4, z: 4, core: 2. Of those that a mesh axis runs over, the one named last changes fastest.
Arguments:
- queries: bfloat16 [8192, 8192], P('seq', 'head'), may hold values from -60 to 60
- keys: bfloat16 [8192, 1024], P('seq', 'head'), may hold values from -6 to 6
- values: bfloat16 [8192, 1024], P('seq', 'head'), may hold values from -6 to 6
- positions: int32 [8192], P('seq'), may hold values from 0 to 8191, as said below
- out_weight: bfloat16 [8192, 8192], P('head', 'seq'), may hold values from -0.25 to 0.25
Outputs:
- mixed: bfloat16 [8192, 8192], P('seq', 'head')
Inputs may be any that keep to these rules, and one draw needn't show every extreme that they name: positions is a permutation of the document's positions; each aligned group of 128 rows holds 128 consecutive positions in increasing order.
All inputs are finite; a program needn't handle non-finite values.
Results may differ from a plain program's by a relative error of at most 0.018.
Values may be sent and summed in bfloat16 or wider, within the bound.
No kernel may reach another device: no remote copies, remote signals or barrier semaphores. Data moves between devices by JAX's collectives and lax.ppermute only.
A program may use at most 128 MiB of HBM per device.

v0:
```python
import functools
import math

import jax
import jax.numpy as jnp
from jax import lax
from jax.experimental import pallas as pl
from jax.experimental.pallas import tpu as pltpu
from jax.sharding import Mesh
from jax.sharding import PartitionSpec as P

HD = 128
BLK = 128
TILE = 512
AXES = ("y", "xl", "c", "xh", "z")
SIZES = {"y": 4, "xl": 2, "c": 2, "xh": 2, "z": 4}
masked_score = -1e30
VMEM_BYTES = 56 << 20


def move(block, axes, target):
    sizes = [SIZES[a] for a in axes]
    count = math.prod(sizes)
    route = []
    for i in range(count):
        rest, at = i, []
        for size in reversed(sizes):
            at.append(rest % size)
            rest //= size
        to = target(*reversed(at))
        j = 0
        for t, size in zip(to, sizes):
            j = j * size + t % size
        route.append((i, j))
    return lax.ppermute(block, axes, route)


def run_all(copies):
    for copy in copies:
        copy.start()
    for copy in copies:
        copy.wait()


def sort_blocks(slot_ref, mine_ref, other_ref, sorted_ref, sem):
    run_all(
        [
            pltpu.make_async_copy(
                (mine_ref, other_ref)[i // 32].at[i // 4 % 8, pl.ds(i % 4 * 2 * BLK, 2 * BLK), :],
                sorted_ref.at[slot_ref[i]],
                sem.at[i],
            )
            for i in range(64)
        ]
    )


def sorted_kv(slots, mine, other):
    anywhere = pl.BlockSpec(memory_space=pl.ANY)
    return pl.pallas_call(
        sort_blocks,
        out_shape=jax.ShapeDtypeStruct((64, 2 * BLK, HD), jnp.bfloat16),
        in_specs=[pl.BlockSpec(memory_space=pltpu.SMEM), anywhere, anywhere],
        out_specs=pl.BlockSpec(memory_space=pltpu.VMEM),
        scratch_shapes=[pltpu.SemaphoreType.DMA((64,))],
        compiler_params=pltpu.CompilerParams(vmem_limit_bytes=VMEM_BYTES),
        cost_estimate=pl.CostEstimate(flops=0, bytes_accessed=8 << 20, transcendentals=0),
        name="sort_blocks",
    )(slots, mine, other)


def attend(chunk, heads, own_ref, order_ref, q_ref, kv_ref, out_ref, kv_s, q_s, s_s, acc, best, total, sem):
    rows = heads * BLK
    tile = TILE * 8 // heads
    per_tile = tile // BLK
    factor = math.log2(math.e) / math.sqrt(HD)
    block = own_ref[order_ref[chunk]]
    tiles = block // per_tile + 1

    def copy_of(j):
        slots = pl.ds(j * per_tile, per_tile)
        return pltpu.make_async_copy(kv_ref.at[slots], kv_s.at[slots], sem.at[j])

    def begin(j, carry):
        copy_of(j).start()
        return carry

    lax.fori_loop(0, tiles, begin, 0)
    for h in range(heads):
        q_s[h * BLK : (h + 1) * BLK, :] = q_ref[:, h * HD : (h + 1) * HD]
    acc[...] = jnp.zeros_like(acc)
    best[...] = jnp.full_like(best, masked_score)
    total[...] = jnp.zeros_like(total)

    def score(j):
        return lax.dot_general(
            kv_s[pl.ds(j * per_tile, per_tile), :BLK, :].reshape(tile, HD),
            q_s[...],
            (((1,), (1,)), ((), ())),
            preferred_element_type=jnp.float32,
        )

    def absorb(j, scores):
        old = best[...]
        new = jnp.maximum(old, jnp.max(scores, axis=0, keepdims=True))
        weights = jnp.exp2((scores - new) * factor)
        shrink = jnp.exp2((old - new) * factor)
        total[...] = total[...] * shrink + jnp.sum(weights, axis=0, keepdims=True)
        best[...] = new
        acc[...] = acc[...] * shrink + lax.dot_general(
            kv_s[pl.ds(j * per_tile, per_tile), BLK:, :].reshape(tile, HD),
            weights.astype(jnp.bfloat16),
            (((0,), (0,)), ((), ())),
            preferred_element_type=jnp.float32,
        )

    copy_of(0).wait()
    s_s[0] = score(0)

    def full_tile(j, carry):
        copy_of(j + 1).wait()
        scores = s_s[j % 2]
        s_s[(j + 1) % 2] = score(j + 1)
        absorb(j, scores)
        return carry

    lax.fori_loop(0, tiles - 1, full_tile, 0)
    last = tiles - 1
    key_at = last * tile + lax.broadcasted_iota(jnp.int32, (tile, rows), 0)
    query_at = block * BLK + lax.broadcasted_iota(jnp.int32, (tile, rows), 1) % BLK
    absorb(last, jnp.where(key_at <= query_at, s_s[last % 2], masked_score))
    result = acc[...] / total[...]
    for h in range(heads):
        part = result[:, h * BLK : (h + 1) * BLK]
        out_ref[:, h * HD : (h + 1) * HD] = part.T.astype(jnp.bfloat16)


def attention(chunk, part, heads, own, order, queries, kv):
    rows = heads * BLK
    tile = TILE * 8 // heads
    return pl.pallas_call(
        functools.partial(attend, chunk, heads),
        out_shape=jax.ShapeDtypeStruct((BLK, heads * HD), jnp.bfloat16),
        grid_spec=pltpu.PrefetchScalarGridSpec(
            num_scalar_prefetch=2,
            grid=(1,),
            in_specs=[
                pl.BlockSpec((BLK, heads * HD), lambda i, own, order: (order[chunk], part)),
                pl.BlockSpec(memory_space=pl.ANY),
            ],
            out_specs=pl.BlockSpec((BLK, heads * HD), lambda i, own, order: (0, 0)),
            scratch_shapes=[
                pltpu.VMEM((64, 2 * BLK, HD), jnp.bfloat16),
                pltpu.VMEM((rows, HD), jnp.bfloat16),
                pltpu.VMEM((2, tile, rows), jnp.float32),
                pltpu.VMEM((HD, rows), jnp.float32),
                pltpu.VMEM((1, rows), jnp.float32),
                pltpu.VMEM((1, rows), jnp.float32),
                pltpu.SemaphoreType.DMA((64 * BLK // tile,)),
            ],
        ),
        compiler_params=pltpu.CompilerParams(vmem_limit_bytes=VMEM_BYTES),
        cost_estimate=pl.CostEstimate(
            flops=1_250_000_000 * heads, bytes_accessed=1 << 22, transcendentals=0
        ),
        name="attend",
    )(own, order, queries, kv)


def project_partner(places, order_ref, *refs):
    pieces, (w_ref, out_ref, all_ref, a_s, sem) = refs[:-5], refs[-5:]
    n = pl.program_id(0)
    keep = pltpu.make_async_copy(a_s, all_ref, sem.at[len(pieces)])

    @pl.when(n == 0)
    def _():
        run_all(
            [
                pltpu.make_async_copy(
                    piece,
                    a_s.at[
                        pl.ds(pl.multiple_of(order_ref[chunk] * BLK, BLK), BLK),
                        pl.ds(at, piece.shape[1]),
                    ],
                    sem.at[i],
                )
                for i, (piece, (chunk, at)) in enumerate(zip(pieces, places))
            ]
        )
        keep.start()

    w = w_ref[...].reshape(4096, 256)
    out = jnp.dot(a_s[...], w, preferred_element_type=jnp.float32)
    out_ref[...] = out.astype(jnp.bfloat16)

    @pl.when(n == pl.num_programs(0) - 1)
    def _():
        keep.wait()


def partner_terms(order, pieces, places, weight):
    return pl.pallas_call(
        functools.partial(project_partner, places),
        out_shape=(
            jax.ShapeDtypeStruct((512, 512), jnp.bfloat16),
            jax.ShapeDtypeStruct((512, 4096), jnp.bfloat16),
        ),
        grid_spec=pltpu.PrefetchScalarGridSpec(
            num_scalar_prefetch=1,
            grid=(2,),
            in_specs=[pl.BlockSpec(memory_space=pl.ANY)] * len(pieces)
            + [pl.BlockSpec((8, None, 512, 256), lambda n, o: (0, 0, 0, n))],
            out_specs=(
                pl.BlockSpec((512, 256), lambda n, o: (0, n)),
                pl.BlockSpec(memory_space=pl.ANY),
            ),
            scratch_shapes=[
                pltpu.VMEM((512, 4096), jnp.bfloat16),
                pltpu.SemaphoreType.DMA((len(pieces) + 1,)),
            ],
        ),
        compiler_params=pltpu.CompilerParams(vmem_limit_bytes=VMEM_BYTES),
        cost_estimate=pl.CostEstimate(
            flops=2 * 512 * 4096 * 512, bytes_accessed=14 << 20, transcendentals=0
        ),
        name="project_partner",
    )(order, *pieces, weight)


def project_rest(a_ref, w_ref, out_ref):
    w = w_ref[...].reshape(4096, 256)
    out = jnp.dot(a_ref[...], w, preferred_element_type=jnp.float32)
    out_ref[...] = out.astype(jnp.bfloat16)


def rest_terms(rows, weight):
    return pl.pallas_call(
        project_rest,
        out_shape=jax.ShapeDtypeStruct((512, 512), jnp.bfloat16),
        grid=(2,),
        in_specs=[
            pl.BlockSpec((512, 4096), lambda n: (0, 0)),
            pl.BlockSpec((8, None, 512, 256), lambda n: (0, 1, 0, n)),
        ],
        out_specs=pl.BlockSpec((512, 256), lambda n: (0, n)),
        compiler_params=pltpu.CompilerParams(vmem_limit_bytes=VMEM_BYTES),
        cost_estimate=pl.CostEstimate(
            flops=2 * 512 * 4096 * 512, bytes_accessed=9 << 20, transcendentals=0
        ),
        name="project_rest",
    )(rows, weight)


def project_self(a_ref, w_ref, first_ref, second_ref, out_ref):
    w = w_ref[...].reshape(4096, 256)
    out = jnp.dot(a_ref[...], w, preferred_element_type=jnp.float32)
    other = jnp.where(pl.program_id(0) < 2, first_ref[...], second_ref[...])
    out_ref[...] = (out + other.astype(jnp.float32)).astype(jnp.bfloat16)


def own_terms(rows, weight, first, second):
    return pl.pallas_call(
        project_self,
        out_shape=jax.ShapeDtypeStruct((512, 1024), jnp.bfloat16),
        grid=(4,),
        in_specs=[
            pl.BlockSpec((512, 4096), lambda n: (0, 0)),
            pl.BlockSpec((8, None, 512, 256), lambda n: (0, n // 2, 0, n % 2)),
            pl.BlockSpec((512, 256), lambda n: (0, jnp.minimum(n, 1))),
            pl.BlockSpec((512, 256), lambda n: (0, jnp.maximum(n - 2, 0))),
        ],
        out_specs=pl.BlockSpec((512, 256), lambda n: (0, n)),
        compiler_params=pltpu.CompilerParams(vmem_limit_bytes=VMEM_BYTES),
        cost_estimate=pl.CostEstimate(
            flops=2 * 512 * 4096 * 1024, bytes_accessed=14 << 20, transcendentals=0
        ),
        name="project_self",
    )(rows, weight, first, second)


def spread_target(half):
    def target(y, xl, xh, z):
        plane = (y % 2) * 2 + xl
        other = (y // 2) ^ xh
        part = half if other else 1 - half
        return ((z - plane) % 4, part, xh, plane)

    return target


def swap_cores(block):
    return move(block, ("c",), lambda a: (a + 1,))


def per_device(queries, keys, values, positions, out_weight):
    y, xl, xh = lax.axis_index("y"), lax.axis_index("xl"), lax.axis_index("xh")
    own = positions[::BLK] // BLK
    index = jnp.arange(4, dtype=jnp.int32)
    rank = jnp.sum((own[None, :] < own[:, None]).astype(jnp.int32), axis=1)
    order = jnp.sum(jnp.where(rank[None, :] == index[:, None], index[None, :], 0), axis=1)
    ids = jnp.broadcast_to(own.astype(jnp.bfloat16)[None, :, None], (4, 4, HD)).reshape(16, HD)
    pairs = jnp.stack([keys.reshape(4, BLK, HD), values.reshape(4, BLK, HD)], 1)
    packet = jnp.concatenate([pairs.reshape(8 * BLK, HD), ids])
    copies = jnp.broadcast_to(packet[None], (8, *packet.shape))
    mine = lax.all_to_all(copies, ("y", "xl"), 0, 0, tiled=True)

    def later(first, *values):
        return lax.optimization_barrier((first, *values))[1:]

    other = (y // 2) ^ xh
    first = lax.dynamic_slice_in_dim(out_weight, (1 - other) * 512, 512, 0)
    second = lax.dynamic_slice_in_dim(out_weight, other * 512, 512, 0)
    plane = ("y", "xl", "xh", "z")
    got_first = move(first, plane, spread_target(0))
    got_second = move(second, plane, spread_target(1))
    got_first, got_second, mine = lax.optimization_barrier((got_first, got_second, mine))
    for_partner = jnp.where(xl == 0, got_first, got_second)
    for_self = jnp.where(xl == 0, got_second, got_first)
    weight_partner = lax.all_gather(for_partner, ("y", "xl", "c")).reshape(8, 2, 512, 512)
    weight_self = lax.all_gather(for_self, ("y", "xl", "c")).reshape(8, 2, 512, 512)

    theirs = swap_cores(mine)
    slots = jnp.concatenate([mine[:, 1024:1028, 0].reshape(32), theirs[:, 1024:1028, 0].reshape(32)])
    kv = sorted_kv(slots.astype(jnp.int32), mine, theirs)
    sets, places = [], []
    for chunk, part, heads in ((0, 0, 8), (1, 0, 8), (2, 0, 8), (3, 0, 4), (3, 1, 4)):
        if sets:
            (queries,) = later(sets[-1][0], queries)
        if len(sets) > 1:
            (queries,) = later(sets[-2][1:], queries)
        piece = attention(chunk, part, heads, own, order, queries, kv)
        around = [move(piece, ("z",), lambda a, dz=dz: (a - dz,)) for dz in (1, 2, 3)]
        sets.append([piece] + around)
        places += [(chunk, dz * 1024 + part * 512) for dz in range(4)]
    pieces = [piece for group in sets for piece in group]
    first_sum, rows = partner_terms(order, pieces, tuple(places), weight_partner)
    got_first = move(first_sum, ("xh",), lambda a: (a + 1,))
    second_sum = rest_terms(rows, weight_partner)
    got_second = move(second_sum, ("xh",), lambda a: (a + 1,))
    return own_terms(rows, weight_self, got_first, got_second)


def solution(mesh):
    split = Mesh(mesh.devices.reshape([SIZES[a] for a in AXES]), AXES)
    seq, head = ("y", "xl", "c"), ("xh", "z")
    placed = (P(seq, head), P(seq, head), P(seq, head), P(seq), P(head, seq))
    return jax.shard_map(
        per_device, mesh=split, in_specs=placed, out_specs=P(seq, head), check_vma=False
    )
```

profile of v0, /device:TPU:25, one launch (start us, length us, event | category | flops | bytes accessed | tf_op | source)
XLA Modules:
  0.0 215.7 jit_solution(17092143309588218223)
XLA Ops:
  6.5 0.8 slice.9
  7.3 0.1 reshape.25
  7.4 1.0 pad_maximum_fusion.1
  8.5 0.2 pad_maximum_fusion
  8.7 1.6 broadcast_in_dim.38
  10.3 5.2 %all-to-all-start = ((bf16[8,1040,128]{2,1,0:T(8,128)(2,1)}), bf16[8,1040,128]{2,1,0:T(8,128)(2,1)S(1)}, u32[]{:S(2)}, u32[]{:S(2)}) async-start(bf16[8,1040,128]{2,1,0:T(8,128)(2,1)} %broadcast_in_dim.38), calls=%async_computation | async-start | bytes 4259840 | tf_op jit(solution)/shard_map/all_to_all | solution.py:305
  15.5 1.1 constant_dynamic-slice_fusion
  16.6 5.8 %collective-permute-start = (bf16[512,512]{1,0:T(8,128)(2,1)}, bf16[512,512]{1,0:T(8,128)(2,1)S(1)}, u32[]{:S(2)}, u32[]{:S(2)}) collective-permute-start(bf16[512,512]{1,0:T(8,128)(2,1)} %get-tuple-element.34), channel_id=1, source_target_pairs={{0,16},{1,48},{2,80},{3,112},{4,4},{5,36},{6,68},{7,100},{16,113},... | collective-permute-start | bytes 1572872 | tf_op jit(solution)/shard_map/ppermute | solution.py:35
  22.4 2.8 %collective-permute-start.1 = (bf16[512,512]{1,0:T(8,128)(2,1)}, bf16[512,512]{1,0:T(8,128)(2,1)S(1)}, u32[]{:S(2)}, u32[]{:S(2)}) collective-permute-start(bf16[512,512]{1,0:T(8,128)(2,1)} %get-tuple-element.33), channel_id=1, source_target_pairs={{0,0},{1,32},{2,64},{3,96},{4,20},{5,52},{6,84},{7,116},{16,97},{1... | collective-permute-start | bytes 1572872 | tf_op jit(solution)/shard_map/ppermute | solution.py:35
  25.2 37.8 %collective-permute-done = bf16[512,512]{1,0:T(8,128)(2,1)S(1)} collective-permute-done((bf16[512,512]{1,0:T(8,128)(2,1)}, bf16[512,512]{1,0:T(8,128)(2,1)S(1)}, u32[]{:S(2)}, u32[]{:S(2)}) %collective-permute-start) | collective-permute-done | bytes 524320 | tf_op jit(solution)/shard_map/ppermute | solution.py:35
  63.0 0.0 collective-permute-done.1
  63.0 0.0 all-to-all-done.mine_ref
  63.0 1.2 broadcast_select_fusion
  64.2 0.0 all-gather.5.cloned.1.call-update
  64.2 0.0 all-gather.7.cloned.1.call-start
  64.3 0.7 all-gather.7.cloned.1.call-update
  65.0 2.0 collective-permute-start.2
  67.0 0.2 convert_reduce_fusion
  67.2 0.7 select_reduce_fusion.order_ref
  67.9 0.1 slice_reduce_fusion.1
  68.0 0.1 reshape_squeeze.6
  68.1 2.9 %collective-permute-done.2.other_ref = bf16[8,1040,128]{2,1,0:T(8,128)(2,1)} collective-permute-done((bf16[8,1040,128]{2,1,0:T(8,128)(2,1)S(1)}, bf16[8,1040,128]{2,1,0:T(8,128)(2,1)}, u32[]{:S(2)}, u32[]{:S(2)}) %collective-permute-start.2) | collective-permute-done | bytes 2129952 | tf_op jit(solution)/shard_map/ppermute | solution.py:35
  71.0 0.8 slice_reduce_fusion
  71.8 0.1 reshape_squeeze.7
  71.9 0.7 maximum_convert_fusion.slot_ref
  72.5 5.4 %sort_blocks.1.kv_ref = bf16[64,256,128]{2,1,0:T(8,128)(2,1)} custom-call(s32[64]{0:T(128)} %maximum_convert_fusion.slot_ref, bf16[8,1040,128]{2,1,0:T(8,128)(2,1)} %copy-done, bf16[8,1040,128]{2,1,0:T(8,128)(2,1)} %collective-permute-done.2.other_ref), custom_call_target="tpu_custom_call" | custom-call | bytes 8388608 | tf_op jit(solution)/shard_map/sort_blocks/pallas_call | solution.py:60
  77.9 8.1 %attend.5.refs_0_ = bf16[128,1024]{1,0:T(8,128)(2,1)} custom-call(s32[4]{0:T(128)} %copy-done.20, s32[4]{0:T(128)} %select_reduce_fusion.order_ref, bf16[512,1024]{1,0:T(8,128)(2,1)} %q_ref.5, bf16[64,256,128]{2,1,0:T(8,128)(2,1)} %sort_blocks.1.kv_ref), custom_call_target="tpu_custom_call" | custom-call | flops 10000000000 | bytes 4194304 | tf_op jit(solution)/shard_map/attend/pallas_call | solution.py:141
  86.1 2.1 collective-permute-start.3
  88.1 0.7 collective-permute-start.5
  88.8 13.9 %attend.6.refs_4_ = bf16[128,1024]{1,0:T(8,128)(2,1)} custom-call(s32[4]{0:T(128)} %copy-done.20, s32[4]{0:T(128)} %select_reduce_fusion.order_ref, bf16[512,1024]{1,0:T(8,128)(2,1)} %q_ref.5, bf16[64,256,128]{2,1,0:T(8,128)(2,1)} %sort_blocks.1.kv_ref), custom_call_target="tpu_custom_call" | custom-call | flops 10000000000 | bytes 4194304 | tf_op jit(solution)/shard_map/attend/pallas_call | solution.py:141
  102.7 2.1 collective-permute-start.6
  104.8 1.8 collective-permute-start.7
  106.5 0.0 collective-permute-done.3.refs_1_
  106.5 0.0 collective-permute-start.8
  106.6 0.0 collective-permute-done.5.refs_3_
  106.6 13.9 %attend.7.refs_8_ = bf16[128,1024]{1,0:T(8,128)(2,1)} custom-call(s32[4]{0:T(128)} %copy-done.20, s32[4]{0:T(128)} %select_reduce_fusion.order_ref, bf16[512,1024]{1,0:T(8,128)(2,1)} %q_ref.5, bf16[64,256,128]{2,1,0:T(8,128)(2,1)} %sort_blocks.1.kv_ref), custom_call_target="tpu_custom_call" | custom-call | flops 10000000000 | bytes 4194304 | tf_op jit(solution)/shard_map/attend/pallas_call | solution.py:141
  120.5 1.9 collective-permute-start.10
  122.4 1.4 collective-permute-start.11
  123.8 0.0 collective-permute-done.6.refs_5_
  123.8 1.3 collective-permute-start.9
  125.1 0.0 collective-permute-done.8.refs_7_
  125.1 9.4 %attend.8.refs_12_ = bf16[128,512]{1,0:T(8,128)(2,1)} custom-call(s32[4]{0:T(128)} %copy-done.20, s32[4]{0:T(128)} %select_reduce_fusion.order_ref, bf16[512,1024]{1,0:T(8,128)(2,1)} %q_ref.5, bf16[64,256,128]{2,1,0:T(8,128)(2,1)} %sort_blocks.1.kv_ref), custom_call_target="tpu_custom_call" | custom-call | flops 5000000000 | bytes 4194304 | tf_op jit(solution)/shard_map/attend/pallas_call | solution.py:141
  134.5 0.3 collective-permute-start.12
  134.8 1.8 collective-permute-start.13
  136.6 0.0 collective-permute-done.11.refs_11_
  136.6 0.0 collective-permute-done.9.refs_9_
  136.6 9.2 %attend.9.refs_16_ = bf16[128,512]{1,0:T(8,128)(2,1)} custom-call(s32[4]{0:T(128)} %copy-done.20, s32[4]{0:T(128)} %select_reduce_fusion.order_ref, bf16[512,1024]{1,0:T(8,128)(2,1)} %q_ref.5, bf16[64,256,128]{2,1,0:T(8,128)(2,1)} %sort_blocks.1.kv_ref), custom_call_target="tpu_custom_call" | custom-call | flops 5000000000 | bytes 4194304 | tf_op jit(solution)/shard_map/attend/pallas_call | solution.py:141
  145.9 2.7 %collective-permute-start.15 = (bf16[128,512]{1,0:T(8,128)(2,1)}, bf16[128,512]{1,0:T(8,128)(2,1)S(1)}, u32[]{:S(2)}, u32[]{:S(2)}) collective-permute-start(bf16[128,512]{1,0:T(8,128)(2,1)} %attend.9.refs_16_), channel_id=1, source_target_pairs={{0,3},{1,0},{2,1},{3,2},{4,7},{5,4},{6,5},{7,6},{8,11},{9,8},{10,9... | collective-permute-start | bytes 393224 | tf_op jit(solution)/shard_map/ppermute | solution.py:35
  148.6 0.6 collective-permute-start.16
  149.1 0.0 collective-permute-done.12.refs_13_
  149.1 0.8 collective-permute-start.17
  149.9 2.9 %collective-permute-done.15.refs_17_ = bf16[128,512]{1,0:T(8,128)(2,1)S(1)} collective-permute-done((bf16[128,512]{1,0:T(8,128)(2,1)}, bf16[128,512]{1,0:T(8,128)(2,1)S(1)}, u32[]{:S(2)}, u32[]{:S(2)}) %collective-permute-start.15) | collective-permute-done | bytes 131104 | tf_op jit(solution)/shard_map/ppermute | solution.py:35
  152.8 1.9 collective-permute-done.16.refs_18_
  154.8 1.2 collective-permute-done.17.refs_19_
  156.0 0.6 copy-done.16
  156.7 8.2 %project_partner.1 = (bf16[512,512]{1,0:T(8,128)(2,1)}, bf16[512,4096]{1,0:T(8,128)(2,1)}) custom-call(s32[4]{0:T(128)} %select_reduce_fusion.order_ref, bf16[128,1024]{1,0:T(8,128)(2,1)} %attend.5.refs_0_, bf16[128,1024]{1,0:T(8,128)(2,1)} %copy-done.2, bf16[128,1024]{1,0:T(8,128)(2,1)} %copy-done.3, bf16[128,1024]{1,0:T(8,128)(2,1)} %copy-done.4, ...), custom_call_target="tpu_custom_call" | custom-call | flops 2147483648 | bytes 14680064 | tf_op jit(solution)/shard_map/project_partner/pallas_call | solution.py:202
  164.8 6.3 %project_rest.1 = bf16[512,512]{1,0:T(8,128)(2,1)} custom-call(bf16[512,4096]{1,0:T(8,128)(2,1)} %get-tuple-element.27.a_ref, bf16[8,2,512,512]{3,2,1,0:T(8,128)(2,1)} %bitcast.6), custom_call_target="tpu_custom_call" | custom-call | flops 2147483648 | bytes 9437184 | tf_op jit(solution)/shard_map/project_rest/pallas_call | solution.py:237
  171.2 2.4 %collective-permute-start.19 = (bf16[512,512]{1,0:T(8,128)(2,1)}, bf16[512,512]{1,0:T(8,128)(2,1)S(1)}, u32[]{:S(2)}, u32[]{:S(2)}) collective-permute-start(bf16[512,512]{1,0:T(8,128)(2,1)} %project_rest.1), channel_id=1, source_target_pairs={{0,4},{4,0},{1,5},{5,1},{2,6},{6,2},{3,7},{7,3},{8,12},{12,8},{9,1... | collective-permute-start | bytes 1572872 | tf_op jit(solution)/shard_map/ppermute | solution.py:35
  173.6 0.6 collective-permute-start.18
  174.1 3.0 %all-gather.7.cloned.1.call-done = bf16[8192,512]{1,0:T(8,128)(2,1)} async-done(((bf16[512,512]{1,0:T(8,128)(2,1)}), bf16[8192,512]{1,0:T(8,128)(2,1)}) %all-gather.7.cloned.1.call-update) | async-done | bytes 8388624 | tf_op jit(solution)/shard_map/all_gather | solution.py:320
  177.2 10.3 %collective-permute-done.19.second_ref = bf16[512,512]{1,0:T(8,128)(2,1)S(1)} collective-permute-done((bf16[512,512]{1,0:T(8,128)(2,1)}, bf16[512,512]{1,0:T(8,128)(2,1)S(1)}, u32[]{:S(2)}, u32[]{:S(2)}) %collective-permute-start.19) | collective-permute-done | bytes 524320 | tf_op jit(solution)/shard_map/ppermute | solution.py:35
  187.5 11.2 %collective-permute-done.18.first_ref = bf16[512,512]{1,0:T(8,128)(2,1)S(1)} collective-permute-done((bf16[512,512]{1,0:T(8,128)(2,1)S(1)}, bf16[512,512]{1,0:T(8,128)(2,1)S(1)}, u32[]{:S(2)}, u32[]{:S(2)}) %collective-permute-start.18) | collective-permute-done | bytes 524320 | tf_op jit(solution)/shard_map/ppermute | solution.py:35
  198.7 0.8 copy-done.19
  199.5 9.4 %project_self.1 = bf16[512,1024]{1,0:T(8,128)(2,1)} custom-call(bf16[512,4096]{1,0:T(8,128)(2,1)} %get-tuple-element.27.a_ref, bf16[8,2,512,512]{3,2,1,0:T(8,128)(2,1)} %bitcast.10, bf16[512,512]{1,0:T(8,128)(2,1)} %copy-done.19, bf16[512,512]{1,0:T(8,128)(2,1)} %copy-done.18), custom_call_target="tpu_custom_call" | custom-call | flops 4294967296 | bytes 14680064 | tf_op jit(solution)/shard_map/project_self/pallas_call | solution.py:262
  (53 shorter events, 0.1 us)
Async XLA Ops:
  7.3 59.7 %copy-start.20 = (s32[4]{0:T(128)}, s32[4]{0:T(128)S(1)}, u32[]{:S(2)}) copy-start(s32[4]{0:T(128)S(1)} %get-tuple-element.30.own_ref) | copy-start | bytes 52
  10.3 5.2 %copy-start.1 = (bf16[1024,512]{1,0:T(8,128)(2,1)S(1)}, bf16[1024,512]{1,0:T(8,128)(2,1)}, u32[]{:S(2)}) copy-start(bf16[1024,512]{1,0:T(8,128)(2,1)} %param.9) | copy-start | bytes 3145732
  10.3 52.7 %all-to-all-start = ((bf16[8,1040,128]{2,1,0:T(8,128)(2,1)}), bf16[8,1040,128]{2,1,0:T(8,128)(2,1)S(1)}, u32[]{:S(2)}, u32[]{:S(2)}) async-start(bf16[8,1040,128]{2,1,0:T(8,128)(2,1)} %broadcast_in_dim.38), calls=%async_computation | async-start | bytes 4259840 | tf_op jit(solution)/shard_map/all_to_all | solution.py:305
  15.5 140.5 %all-gather.5.cloned.1.call-start = ((), (), s32[]{:S(2)}) async-start(), calls=%async_computation.1 | async-start | bytes 8912896 | tf_op jit(solution)/shard_map/all_gather | solution.py:319
  16.6 46.4 %collective-permute-start = (bf16[512,512]{1,0:T(8,128)(2,1)}, bf16[512,512]{1,0:T(8,128)(2,1)S(1)}, u32[]{:S(2)}, u32[]{:S(2)}) collective-permute-start(bf16[512,512]{1,0:T(8,128)(2,1)} %get-tuple-element.34), channel_id=1, source_target_pairs={{0,16},{1,48},{2,80},{3,112},{4,4},{5,36},{6,68},{7,100},{16,113},... | collective-permute-start | bytes 1572872 | tf_op jit(solution)/shard_map/ppermute | solution.py:35
  22.4 40.6 %collective-permute-start.1 = (bf16[512,512]{1,0:T(8,128)(2,1)}, bf16[512,512]{1,0:T(8,128)(2,1)S(1)}, u32[]{:S(2)}, u32[]{:S(2)}) collective-permute-start(bf16[512,512]{1,0:T(8,128)(2,1)} %get-tuple-element.33), channel_id=1, source_target_pairs={{0,0},{1,32},{2,64},{3,96},{4,20},{5,52},{6,84},{7,116},{16,97},{1... | collective-permute-start | bytes 1572872 | tf_op jit(solution)/shard_map/ppermute | solution.py:35
  63.0 9.5 %copy-start = (bf16[8,1040,128]{2,1,0:T(8,128)(2,1)}, bf16[8,1040,128]{2,1,0:T(8,128)(2,1)S(1)}, u32[]{:S(2)}) copy-start(bf16[8,1040,128]{2,1,0:T(8,128)(2,1)S(1)} %all-to-all-done.mine_ref) | copy-start | bytes 6389764
  64.2 112.9 %all-gather.7.cloned.1.call-start = ((), (), s32[]{:S(2)}) async-start(), calls=%async_computation.2 | async-start | bytes 8912896 | tf_op jit(solution)/shard_map/all_gather | solution.py:320
  65.0 6.0 %collective-permute-start.2 = (bf16[8,1040,128]{2,1,0:T(8,128)(2,1)S(1)}, bf16[8,1040,128]{2,1,0:T(8,128)(2,1)}, u32[]{:S(2)}, u32[]{:S(2)}) collective-permute-start(bf16[8,1040,128]{2,1,0:T(8,128)(2,1)S(1)} %all-to-all-done.mine_ref), channel_id=1, source_target_pairs={{0,8},{8,0},{1,9},{9,1},{2,10},{10,2},{3,11},{11,3},{4,12},{12,4},... | collective-permute-start | bytes 6389768 | tf_op jit(solution)/shard_map/ppermute | solution.py:35
  86.1 20.5 %collective-permute-start.3 = (bf16[128,1024]{1,0:T(8,128)(2,1)}, bf16[128,1024]{1,0:T(8,128)(2,1)S(1)}, u32[]{:S(2)}, u32[]{:S(2)}) collective-permute-start(bf16[128,1024]{1,0:T(8,128)(2,1)} %attend.5.refs_0_), channel_id=1, source_target_pairs={{0,3},{1,0},{2,1},{3,2},{4,7},{5,4},{6,5},{7,6},{8,11},{9,8},{10,9... | collective-permute-start | bytes 786440 | tf_op jit(solution)/shard_map/ppermute | solution.py:35
  88.1 18.4 %collective-permute-start.4 = (bf16[128,1024]{1,0:T(8,128)(2,1)}, bf16[128,1024]{1,0:T(8,128)(2,1)S(1)}, u32[]{:S(2)}, u32[]{:S(2)}) collective-permute-start(bf16[128,1024]{1,0:T(8,128)(2,1)} %attend.5.refs_0_), channel_id=1, source_target_pairs={{0,2},{1,3},{2,0},{3,1},{4,6},{5,7},{6,4},{7,5},{8,10},{9,11},{10,... | collective-permute-start | bytes 786440 | tf_op jit(solution)/shard_map/ppermute | solution.py:35
  88.1 18.4 %collective-permute-start.5 = (bf16[128,1024]{1,0:T(8,128)(2,1)}, bf16[128,1024]{1,0:T(8,128)(2,1)S(1)}, u32[]{:S(2)}, u32[]{:S(2)}) collective-permute-start(bf16[128,1024]{1,0:T(8,128)(2,1)} %attend.5.refs_0_), channel_id=1, source_target_pairs={{0,1},{1,2},{2,3},{3,0},{4,5},{5,6},{6,7},{7,4},{8,9},{9,10},{10,1... | collective-permute-start | bytes 786440 | tf_op jit(solution)/shard_map/ppermute | solution.py:35
  102.7 21.1 %collective-permute-start.6 = (bf16[128,1024]{1,0:T(8,128)(2,1)}, bf16[128,1024]{1,0:T(8,128)(2,1)S(1)}, u32[]{:S(2)}, u32[]{:S(2)}) collective-permute-start(bf16[128,1024]{1,0:T(8,128)(2,1)} %attend.6.refs_4_), channel_id=1, source_target_pairs={{0,3},{1,0},{2,1},{3,2},{4,7},{5,4},{6,5},{7,6},{8,11},{9,8},{10,9... | collective-permute-start | bytes 786440 | tf_op jit(solution)/shard_map/ppermute | solution.py:35
  104.8 20.4 %collective-permute-start.7 = (bf16[128,1024]{1,0:T(8,128)(2,1)}, bf16[128,1024]{1,0:T(8,128)(2,1)S(1)}, u32[]{:S(2)}, u32[]{:S(2)}) collective-permute-start(bf16[128,1024]{1,0:T(8,128)(2,1)} %attend.6.refs_4_), channel_id=1, source_target_pairs={{0,2},{1,3},{2,0},{3,1},{4,6},{5,7},{6,4},{7,5},{8,10},{9,11},{10,... | collective-permute-start | bytes 786440 | tf_op jit(solution)/shard_map/ppermute | solution.py:35
  106.5 13.9 %copy-start.2 = (bf16[128,1024]{1,0:T(8,128)(2,1)}, bf16[128,1024]{1,0:T(8,128)(2,1)S(1)}, u32[]{:S(2)}) copy-start(bf16[128,1024]{1,0:T(8,128)(2,1)S(1)} %collective-permute-done.3.refs_1_) | copy-start | bytes 786436
  106.5 18.6 %collective-permute-start.8 = (bf16[128,1024]{1,0:T(8,128)(2,1)}, bf16[128,1024]{1,0:T(8,128)(2,1)S(1)}, u32[]{:S(2)}, u32[]{:S(2)}) collective-permute-start(bf16[128,1024]{1,0:T(8,128)(2,1)} %attend.6.refs_4_), channel_id=1, source_target_pairs={{0,1},{1,2},{2,3},{3,0},{4,5},{5,6},{6,7},{7,4},{8,9},{9,10},{10,1... | collective-permute-start | bytes 786440 | tf_op jit(solution)/shard_map/ppermute | solution.py:35
  106.5 13.9 %copy-start.3 = (bf16[128,1024]{1,0:T(8,128)(2,1)}, bf16[128,1024]{1,0:T(8,128)(2,1)S(1)}, u32[]{:S(2)}) copy-start(bf16[128,1024]{1,0:T(8,128)(2,1)S(1)} %collective-permute-done.4.refs_2_) | copy-start | bytes 786436
  106.6 13.9 %copy-start.4 = (bf16[128,1024]{1,0:T(8,128)(2,1)}, bf16[128,1024]{1,0:T(8,128)(2,1)S(1)}, u32[]{:S(2)}) copy-start(bf16[128,1024]{1,0:T(8,128)(2,1)S(1)} %collective-permute-done.5.refs_3_) | copy-start | bytes 786436
  120.5 16.1 %collective-permute-start.10 = (bf16[128,1024]{1,0:T(8,128)(2,1)}, bf16[128,1024]{1,0:T(8,128)(2,1)S(1)}, u32[]{:S(2)}, u32[]{:S(2)}) collective-permute-start(bf16[128,1024]{1,0:T(8,128)(2,1)} %attend.7.refs_8_), channel_id=1, source_target_pairs={{0,2},{1,3},{2,0},{3,1},{4,6},{5,7},{6,4},{7,5},{8,10},{9,11},{10,... | collective-permute-start | bytes 786440 | tf_op jit(solution)/shard_map/ppermute | solution.py:35
  122.4 14.1 %collective-permute-start.11 = (bf16[128,1024]{1,0:T(8,128)(2,1)}, bf16[128,1024]{1,0:T(8,128)(2,1)S(1)}, u32[]{:S(2)}, u32[]{:S(2)}) collective-permute-start(bf16[128,1024]{1,0:T(8,128)(2,1)} %attend.7.refs_8_), channel_id=1, source_target_pairs={{0,1},{1,2},{2,3},{3,0},{4,5},{5,6},{6,7},{7,4},{8,9},{9,10},{10,1... | collective-permute-start | bytes 786440 | tf_op jit(solution)/shard_map/ppermute | solution.py:35
  123.8 10.7 %copy-start.5 = (bf16[128,1024]{1,0:T(8,128)(2,1)}, bf16[128,1024]{1,0:T(8,128)(2,1)S(1)}, u32[]{:S(2)}) copy-start(bf16[128,1024]{1,0:T(8,128)(2,1)S(1)} %collective-permute-done.6.refs_5_) | copy-start | bytes 786436
  123.8 12.8 %collective-permute-start.9 = (bf16[128,1024]{1,0:T(8,128)(2,1)}, bf16[128,1024]{1,0:T(8,128)(2,1)S(1)}, u32[]{:S(2)}, u32[]{:S(2)}) collective-permute-start(bf16[128,1024]{1,0:T(8,128)(2,1)} %attend.7.refs_8_), channel_id=1, source_target_pairs={{0,3},{1,0},{2,1},{3,2},{4,7},{5,4},{6,5},{7,6},{8,11},{9,8},{10,9... | collective-permute-start | bytes 786440 | tf_op jit(solution)/shard_map/ppermute | solution.py:35
  125.1 9.4 %copy-start.6 = (bf16[128,1024]{1,0:T(8,128)(2,1)}, bf16[128,1024]{1,0:T(8,128)(2,1)S(1)}, u32[]{:S(2)}) copy-start(bf16[128,1024]{1,0:T(8,128)(2,1)S(1)} %collective-permute-done.7.refs_6_) | copy-start | bytes 786436
  125.1 9.4 %copy-start.7 = (bf16[128,1024]{1,0:T(8,128)(2,1)}, bf16[128,1024]{1,0:T(8,128)(2,1)S(1)}, u32[]{:S(2)}) copy-start(bf16[128,1024]{1,0:T(8,128)(2,1)S(1)} %collective-permute-done.8.refs_7_) | copy-start | bytes 786436
  134.5 14.6 %collective-permute-start.12 = (bf16[128,512]{1,0:T(8,128)(2,1)}, bf16[128,512]{1,0:T(8,128)(2,1)S(1)}, u32[]{:S(2)}, u32[]{:S(2)}) collective-permute-start(bf16[128,512]{1,0:T(8,128)(2,1)} %attend.8.refs_12_), channel_id=1, source_target_pairs={{0,3},{1,0},{2,1},{3,2},{4,7},{5,4},{6,5},{7,6},{8,11},{9,8},{10,9... | collective-permute-start | bytes 393224 | tf_op jit(solution)/shard_map/ppermute | solution.py:35
  134.8 15.1 %collective-permute-start.13 = (bf16[128,512]{1,0:T(8,128)(2,1)}, bf16[128,512]{1,0:T(8,128)(2,1)S(1)}, u32[]{:S(2)}, u32[]{:S(2)}) collective-permute-start(bf16[128,512]{1,0:T(8,128)(2,1)} %attend.8.refs_12_), channel_id=1, source_target_pairs={{0,2},{1,3},{2,0},{3,1},{4,6},{5,7},{6,4},{7,5},{8,10},{9,11},{10,... | collective-permute-start | bytes 393224 | tf_op jit(solution)/shard_map/ppermute | solution.py:35
  136.6 9.3 %copy-start.8 = (bf16[128,1024]{1,0:T(8,128)(2,1)}, bf16[128,1024]{1,0:T(8,128)(2,1)S(1)}, u32[]{:S(2)}) copy-start(bf16[128,1024]{1,0:T(8,128)(2,1)S(1)} %collective-permute-done.10.refs_10_) | copy-start | bytes 786436
  136.6 13.3 %collective-permute-start.14 = (bf16[128,512]{1,0:T(8,128)(2,1)}, bf16[128,512]{1,0:T(8,128)(2,1)S(1)}, u32[]{:S(2)}, u32[]{:S(2)}) collective-permute-start(bf16[128,512]{1,0:T(8,128)(2,1)} %attend.8.refs_12_), channel_id=1, source_target_pairs={{0,1},{1,2},{2,3},{3,0},{4,5},{5,6},{6,7},{7,4},{8,9},{9,10},{10,1... | collective-permute-start | bytes 393224 | tf_op jit(solution)/shard_map/ppermute | solution.py:35
  136.6 9.2 %copy-start.9 = (bf16[128,1024]{1,0:T(8,128)(2,1)}, bf16[128,1024]{1,0:T(8,128)(2,1)S(1)}, u32[]{:S(2)}) copy-start(bf16[128,1024]{1,0:T(8,128)(2,1)S(1)} %collective-permute-done.11.refs_11_) | copy-start | bytes 786436
  136.6 9.2 %copy-start.10 = (bf16[128,1024]{1,0:T(8,128)(2,1)}, bf16[128,1024]{1,0:T(8,128)(2,1)S(1)}, u32[]{:S(2)}) copy-start(bf16[128,1024]{1,0:T(8,128)(2,1)S(1)} %collective-permute-done.9.refs_9_) | copy-start | bytes 786436
  145.9 7.0 %collective-permute-start.15 = (bf16[128,512]{1,0:T(8,128)(2,1)}, bf16[128,512]{1,0:T(8,128)(2,1)S(1)}, u32[]{:S(2)}, u32[]{:S(2)}) collective-permute-start(bf16[128,512]{1,0:T(8,128)(2,1)} %attend.9.refs_16_), channel_id=1, source_target_pairs={{0,3},{1,0},{2,1},{3,2},{4,7},{5,4},{6,5},{7,6},{8,11},{9,8},{10,9... | collective-permute-start | bytes 393224 | tf_op jit(solution)/shard_map/ppermute | solution.py:35
  148.6 6.2 %collective-permute-start.16 = (bf16[128,512]{1,0:T(8,128)(2,1)}, bf16[128,512]{1,0:T(8,128)(2,1)S(1)}, u32[]{:S(2)}, u32[]{:S(2)}) collective-permute-start(bf16[128,512]{1,0:T(8,128)(2,1)} %attend.9.refs_16_), channel_id=1, source_target_pairs={{0,2},{1,3},{2,0},{3,1},{4,6},{5,7},{6,4},{7,5},{8,10},{9,11},{10,... | collective-permute-start | bytes 393224 | tf_op jit(solution)/shard_map/ppermute | solution.py:35
  149.1 6.9 %copy-start.11 = (bf16[128,512]{1,0:T(8,128)(2,1)}, bf16[128,512]{1,0:T(8,128)(2,1)S(1)}, u32[]{:S(2)}) copy-start(bf16[128,512]{1,0:T(8,128)(2,1)S(1)} %collective-permute-done.12.refs_13_) | copy-start | bytes 393220
  149.1 6.9 %collective-permute-start.17 = (bf16[128,512]{1,0:T(8,128)(2,1)}, bf16[128,512]{1,0:T(8,128)(2,1)S(1)}, u32[]{:S(2)}, u32[]{:S(2)}) collective-permute-start(bf16[128,512]{1,0:T(8,128)(2,1)} %attend.9.refs_16_), channel_id=1, source_target_pairs={{0,1},{1,2},{2,3},{3,0},{4,5},{5,6},{6,7},{7,4},{8,9},{9,10},{10,1... | collective-permute-start | bytes 393224 | tf_op jit(solution)/shard_map/ppermute | solution.py:35
  149.9 6.1 %copy-start.12 = (bf16[128,512]{1,0:T(8,128)(2,1)}, bf16[128,512]{1,0:T(8,128)(2,1)S(1)}, u32[]{:S(2)}) copy-start(bf16[128,512]{1,0:T(8,128)(2,1)S(1)} %collective-permute-done.13.refs_14_) | copy-start | bytes 393220
  149.9 6.1 %copy-start.13 = (bf16[128,512]{1,0:T(8,128)(2,1)}, bf16[128,512]{1,0:T(8,128)(2,1)S(1)}, u32[]{:S(2)}) copy-start(bf16[128,512]{1,0:T(8,128)(2,1)S(1)} %collective-permute-done.14.refs_15_) | copy-start | bytes 393220
  152.8 3.2 %copy-start.14 = (bf16[128,512]{1,0:T(8,128)(2,1)}, bf16[128,512]{1,0:T(8,128)(2,1)S(1)}, u32[]{:S(2)}) copy-start(bf16[128,512]{1,0:T(8,128)(2,1)S(1)} %collective-permute-done.15.refs_17_) | copy-start | bytes 393220
  154.8 1.3 copy-start.15
  156.0 0.6 copy-start.16
  164.8 8.7 %copy-start.17 = (bf16[512,512]{1,0:T(8,128)(2,1)S(1)}, bf16[512,512]{1,0:T(8,128)(2,1)}, u32[]{:S(2)}) copy-start(bf16[512,512]{1,0:T(8,128)(2,1)} %get-tuple-element.28) | copy-start | bytes 1572868
  171.2 16.3 %collective-permute-start.19 = (bf16[512,512]{1,0:T(8,128)(2,1)}, bf16[512,512]{1,0:T(8,128)(2,1)S(1)}, u32[]{:S(2)}, u32[]{:S(2)}) collective-permute-start(bf16[512,512]{1,0:T(8,128)(2,1)} %project_rest.1), channel_id=1, source_target_pairs={{0,4},{4,0},{1,5},{5,1},{2,6},{6,2},{3,7},{7,3},{8,12},{12,8},{9,1... | collective-permute-start | bytes 1572872 | tf_op jit(solution)/shard_map/ppermute | solution.py:35
  173.6 25.2 %collective-permute-start.18 = (bf16[512,512]{1,0:T(8,128)(2,1)S(1)}, bf16[512,512]{1,0:T(8,128)(2,1)S(1)}, u32[]{:S(2)}, u32[]{:S(2)}) collective-permute-start(bf16[512,512]{1,0:T(8,128)(2,1)S(1)} %copy-done.17), channel_id=1, source_target_pairs={{0,4},{4,0},{1,5},{5,1},{2,6},{6,2},{3,7},{7,3},{8,12},{12,8},{9,1... | collective-permute-start | bytes 1572872 | tf_op jit(solution)/shard_map/ppermute | solution.py:35
  187.5 11.2 %copy-start.18 = (bf16[512,512]{1,0:T(8,128)(2,1)}, bf16[512,512]{1,0:T(8,128)(2,1)S(1)}, u32[]{:S(2)}) copy-start(bf16[512,512]{1,0:T(8,128)(2,1)S(1)} %collective-permute-done.19.second_ref) | copy-start | bytes 1572868
  198.7 0.8 copy-start.19
Sparse Core Ops, SparseCore 0:
  64.4 57.3 all-gather.4
  123.5 53.6 all-gather.6
where the time goes:
time: 217 us; the launch traced here: 216 us
  Pallas kernels  83.7 us (39%)
  waiting for transfers between devices  72.1 us (33%)
  starting transfers between devices  36.1 us (17%)
  between operations  13.8 us (6%)
  local copies, waits for them, and re-layouts  6.17 us (3%)
  other arithmetic  3.96 us (2%)
    ppermute x20, waiting for transfers between devices, move(): return lax.ppermute(block, axes, route)  68.3 us
    pallas_call x5, Pallas kernels, attention(): pl.pallas_call(functools.partial(attend, chunk, heads), out_shape=jax.Sha...  54.5 us
    ppermute x20, starting transfers between devices, move(): return lax.ppermute(block, axes, route)  30.9 us
    pallas_call x1, Pallas kernels, own_terms(): pl.pallas_call(project_self, out_shape=jax.ShapeDtypeStruct((512, 1024),...  9.36 us
    pallas_call x1, Pallas kernels, partner_terms(): pl.pallas_call(functools.partial(project_partner, places), out_shape=(jax...  8.16 us
    pallas_call x1, Pallas kernels, rest_terms(): pl.pallas_call(project_rest, out_shape=jax.ShapeDtypeStruct((512, 512), j...  6.32 us
    pallas_call x1, Pallas kernels, sorted_kv(): pl.pallas_call(sort_blocks, out_shape=jax.ShapeDtypeStruct((64, 2 * BLK,...  5.4 us
    all_to_all x1, starting transfers between devices, per_device(): mine = lax.all_to_all(copies, ('y', 'xl'), 0, 0, tiled=True)  5.19 us
  transfers between devices with their start and end apart: 23, of which 8 were waited for; matrix products, arithmetic and copies ran while one was open for 2% of the time, Pallas kernels for 34%

commit v1 on v0

--- a/solution.py
+++ b/solution.py
@@ -307,18 +307,13 @@
     def later(first, *values):
         return lax.optimization_barrier((first, *values))[1:]
 
+    (out_weight,) = later(mine, out_weight)
     other = (y // 2) ^ xh
     first = lax.dynamic_slice_in_dim(out_weight, (1 - other) * 512, 512, 0)
     second = lax.dynamic_slice_in_dim(out_weight, other * 512, 512, 0)
     plane = ("y", "xl", "xh", "z")
     got_first = move(first, plane, spread_target(0))
     got_second = move(second, plane, spread_target(1))
-    got_first, got_second, mine = lax.optimization_barrier((got_first, got_second, mine))
-    for_partner = jnp.where(xl == 0, got_first, got_second)
-    for_self = jnp.where(xl == 0, got_second, got_first)
-    weight_partner = lax.all_gather(for_partner, ("y", "xl", "c")).reshape(8, 2, 512, 512)
-    weight_self = lax.all_gather(for_self, ("y", "xl", "c")).reshape(8, 2, 512, 512)
-
     theirs = swap_cores(mine)
     slots = jnp.concatenate([mine[:, 1024:1028, 0].reshape(32), theirs[:, 1024:1028, 0].reshape(32)])
     kv = sorted_kv(slots.astype(jnp.int32), mine, theirs)
@@ -331,6 +326,12 @@
         piece = attention(chunk, part, heads, own, order, queries, kv)
         around = [move(piece, ("z",), lambda a, dz=dz: (a - dz,)) for dz in (1, 2, 3)]
         sets.append([piece] + around)
+        if chunk == 0:
+            got_first, got_second = later(piece, got_first, got_second)
+            for_partner = jnp.where(xl == 0, got_first, got_second)
+            for_self = jnp.where(xl == 0, got_second, got_first)
+            weight_partner = lax.all_gather(for_partner, ("y", "xl", "c")).reshape(8, 2, 512, 512)
+            weight_self = lax.all_gather(for_self, ("y", "xl", "c")).reshape(8, 2, 512, 512)
         places += [(chunk, dz * 1024 + part * 512) for dz in range(4)]
     pieces = [piece for group in sets for piece in group]
     first_sum, rows = partner_terms(order, pieces, tuple(places), weight_partner)

time: 217 us -> 226 us (1.041); the launches traced: 216 us -> 222 us
  blocking collectives: 0 us -> 29.8 us
  waiting for transfers between devices: 72.1 us -> 56.4 us
  Pallas kernels: 83.7 us -> 79.3 us
  starting transfers between devices: 36.1 us -> 33.6 us
    ppermute x20, waiting for transfers between devices: 68.3 us -> 10.6 us  [move(): return lax.ppermute(block, axes, route)]
    all_gather x1, waiting for transfers between devices: 3.05 us -> 45.1 us  [per_device(): lax.all_gather(for_self, ('y', 'xl', 'c')).reshape(8, 2, 512, 512)]
    all_to_all x0 -> x1, blocking collectives: none -> 29.8 us  [per_device(): mine = lax.all_to_all(copies, ('y', 'xl'), 0, 0, tiled=True)]
    all_to_all x1 -> x0, starting transfers between devices: 5.19 us -> none  [per_device(): mine = lax.all_to_all(copies, ('y', 'xl'), 0, 0, tiled=True)]
    pallas_call x5, Pallas kernels: 54.5 us -> 50.2 us  [attention(): pl.pallas_call(functools.partial(attend, chunk, heads), out_shape=jax.Sha...]
    ppermute x20, starting transfers between devices: 30.9 us -> 33.6 us  [move(): return lax.ppermute(block, axes, route)]
  transfers between devices with their start and end apart: 23 -> 22, of which waited for: 8 -> 7; matrix products, arithmetic and copies ran while one was open for 2% -> 2% of each run, Pallas kernels for 34% -> 32%
where the time goes in v1:
time: 226 us; the launch traced here: 222 us
  Pallas kernels  79.3 us (35%)
  waiting for transfers between devices  56.4 us (25%)
  starting transfers between devices  33.6 us (15%)
  blocking collectives  29.8 us (13%)
  between operations  13.8 us (6%)
  local copies, waits for them, and re-layouts  4.97 us (2%)
  other arithmetic  3.83 us (2%)
    pallas_call x5, Pallas kernels, attention(): pl.pallas_call(functools.partial(attend, chunk, heads), out_shape=jax.Sha...  50.2 us
    all_gather x1, waiting for transfers between devices, per_device(): lax.all_gather(for_self, ('y', 'xl', 'c')).reshape(8, 2, 512, 512)  45.1 us
    ppermute x20, starting transfers between devices, move(): return lax.ppermute(block, axes, route)  33.6 us
    all_to_all x1, blocking collectives, per_device(): mine = lax.all_to_all(copies, ('y', 'xl'), 0, 0, tiled=True)  29.8 us
    ppermute x20, waiting for transfers between devices, move(): return lax.ppermute(block, axes, route)  10.6 us
    pallas_call x1, Pallas kernels, own_terms(): pl.pallas_call(project_self, out_shape=jax.ShapeDtypeStruct((512, 1024),...  9.36 us
    pallas_call x1, Pallas kernels, partner_terms(): pl.pallas_call(functools.partial(project_partner, places), out_shape=(jax...  8.06 us
    pallas_call x1, Pallas kernels, rest_terms(): pl.pallas_call(project_rest, out_shape=jax.ShapeDtypeStruct((512, 512), j...  6.3 us
  transfers between devices with their start and end apart: 22, of which 7 were waited for; matrix products, arithmetic and copies ran while one was open for 2% of the time, Pallas kernels for 32%

profile of v1, /device:TPU:25, one launch (start us, length us, event | category | flops | bytes accessed | tf_op | source)
XLA Modules:
  0.0 221.6 jit_solution(18150146129324739567)
XLA Ops:
  6.5 0.8 slice.9
  7.3 0.1 reshape.25
  7.4 1.0 pad_maximum_fusion.1
  8.5 0.2 pad_maximum_fusion
  8.7 0.3 broadcast_in_dim.38
  9.0 0.0 copy-start.1
  9.0 29.8 %all_to_all.5.mine_ref = bf16[8,1040,128]{2,1,0:T(8,128)(2,1)S(1)} all-to-all(bf16[8,1040,128]{2,1,0:T(8,128)(2,1)S(1)} %broadcast_in_dim.38), channel_id=1, replica_groups=mesh['y'=4,'xl'=2,'c'=2,'xh'=2,'z'=4] {'y','xl'}, dimensions={0} | all-to-all | bytes 4259840 | tf_op jit(solution)/shard_map/all_to_all | solution.py:305
  38.7 2.2 collective-permute-start
  40.9 0.2 convert_reduce_fusion
  41.1 0.7 select_reduce_fusion.order_ref
  41.8 1.0 constant_dynamic-slice_fusion.1
  42.9 5.5 %collective-permute-start.16 = (bf16[512,512]{1,0:T(8,128)(2,1)}, bf16[512,512]{1,0:T(8,128)(2,1)S(1)}, u32[]{:S(2)}, u32[]{:S(2)}) collective-permute-start(bf16[512,512]{1,0:T(8,128)(2,1)} %get-tuple-element.34), channel_id=1, source_target_pairs={{0,16},{1,48},{2,80},{3,112},{4,4},{5,36},{6,68},{7,100},{16,113},... | collective-permute-start | bytes 1572872 | tf_op jit(solution)/shard_map/ppermute | solution.py:35
  48.4 3.5 %collective-permute-start.17 = (bf16[512,512]{1,0:T(8,128)(2,1)}, bf16[512,512]{1,0:T(8,128)(2,1)S(1)}, u32[]{:S(2)}, u32[]{:S(2)}) collective-permute-start(bf16[512,512]{1,0:T(8,128)(2,1)} %get-tuple-element.33), channel_id=1, source_target_pairs={{0,0},{1,32},{2,64},{3,96},{4,20},{5,52},{6,84},{7,116},{16,97},{1... | collective-permute-start | bytes 1572872 | tf_op jit(solution)/shard_map/ppermute | solution.py:35
  51.9 0.1 slice_reduce_fusion.1
  52.0 0.1 reshape_squeeze.6
  52.1 0.0 collective-permute-done.other_ref
  52.1 0.8 slice_reduce_fusion
  52.9 0.1 reshape_squeeze.7
  53.0 0.7 maximum_convert_fusion.slot_ref
  53.7 5.4 %sort_blocks.1.kv_ref = bf16[64,256,128]{2,1,0:T(8,128)(2,1)} custom-call(s32[64]{0:T(128)} %maximum_convert_fusion.slot_ref, bf16[8,1040,128]{2,1,0:T(8,128)(2,1)} %copy-done, bf16[8,1040,128]{2,1,0:T(8,128)(2,1)} %collective-permute-done.other_ref), custom_call_target="tpu_custom_call" | custom-call | bytes 8388608 | tf_op jit(solution)/shard_map/sort_blocks/pallas_call | solution.py:60
  59.1 8.1 %attend.5.refs_0_ = bf16[128,1024]{1,0:T(8,128)(2,1)} custom-call(s32[4]{0:T(128)} %copy-done.21, s32[4]{0:T(128)} %select_reduce_fusion.order_ref, bf16[512,1024]{1,0:T(8,128)(2,1)} %q_ref.5, bf16[64,256,128]{2,1,0:T(8,128)(2,1)} %sort_blocks.1.kv_ref), custom_call_target="tpu_custom_call" | custom-call | flops 10000000000 | bytes 4194304 | tf_op jit(solution)/shard_map/attend/pallas_call | solution.py:141
  67.2 3.8 %collective-permute-done.16 = bf16[512,512]{1,0:T(8,128)(2,1)S(1)} collective-permute-done((bf16[512,512]{1,0:T(8,128)(2,1)}, bf16[512,512]{1,0:T(8,128)(2,1)S(1)}, u32[]{:S(2)}, u32[]{:S(2)}) %collective-permute-start.16) | collective-permute-done | bytes 524320 | tf_op jit(solution)/shard_map/ppermute | solution.py:35
  71.0 0.4 collective-permute-done.17
  71.4 1.1 broadcast_select_fusion
  72.5 0.0 all-gather.5.cloned.1.call-update
  72.5 0.0 all-gather.7.cloned.1.call-start
  72.5 0.7 all-gather.7.cloned.1.call-update
  73.2 2.2 collective-permute-start.1
  75.4 0.8 collective-permute-start.2
  76.2 0.0 collective-permute-start.3
  76.2 10.6 %attend.6.refs_4_ = bf16[128,1024]{1,0:T(8,128)(2,1)} custom-call(s32[4]{0:T(128)} %copy-done.21, s32[4]{0:T(128)} %select_reduce_fusion.order_ref, bf16[512,1024]{1,0:T(8,128)(2,1)} %q_ref.5, bf16[64,256,128]{2,1,0:T(8,128)(2,1)} %sort_blocks.1.kv_ref), custom_call_target="tpu_custom_call" | custom-call | flops 10000000000 | bytes 4194304 | tf_op jit(solution)/shard_map/attend/pallas_call | solution.py:141
  86.8 2.7 %collective-permute-start.4 = (bf16[128,1024]{1,0:T(8,128)(2,1)}, bf16[128,1024]{1,0:T(8,128)(2,1)S(1)}, u32[]{:S(2)}, u32[]{:S(2)}) collective-permute-start(bf16[128,1024]{1,0:T(8,128)(2,1)} %attend.6.refs_4_), channel_id=1, source_target_pairs={{0,3},{1,0},{2,1},{3,2},{4,7},{5,4},{6,5},{7,6},{8,11},{9,8},{10,9... | collective-permute-start | bytes 786440 | tf_op jit(solution)/shard_map/ppermute | solution.py:35
  89.5 1.0 collective-permute-start.5
  90.5 0.0 collective-permute-done.1.refs_1_
  90.5 0.0 collective-permute-start.6
  90.5 0.0 collective-permute-done.2.refs_2_
  90.5 0.2 collective-permute-done.3.refs_3_
  90.8 11.4 %attend.7.refs_8_ = bf16[128,1024]{1,0:T(8,128)(2,1)} custom-call(s32[4]{0:T(128)} %copy-done.21, s32[4]{0:T(128)} %select_reduce_fusion.order_ref, bf16[512,1024]{1,0:T(8,128)(2,1)} %q_ref.5, bf16[64,256,128]{2,1,0:T(8,128)(2,1)} %sort_blocks.1.kv_ref), custom_call_target="tpu_custom_call" | custom-call | flops 10000000000 | bytes 4194304 | tf_op jit(solution)/shard_map/attend/pallas_call | solution.py:141
  102.2 2.5 %collective-permute-start.7 = (bf16[128,1024]{1,0:T(8,128)(2,1)}, bf16[128,1024]{1,0:T(8,128)(2,1)S(1)}, u32[]{:S(2)}, u32[]{:S(2)}) collective-permute-start(bf16[128,1024]{1,0:T(8,128)(2,1)} %attend.7.refs_8_), channel_id=1, source_target_pairs={{0,3},{1,0},{2,1},{3,2},{4,7},{5,4},{6,5},{7,6},{8,11},{9,8},{10,9... | collective-permute-start | bytes 786440 | tf_op jit(solution)/shard_map/ppermute | solution.py:35
  104.7 0.8 collective-permute-start.8
  105.5 0.0 collective-permute-done.4.refs_5_
  105.5 0.0 collective-permute-start.9
  105.6 10.2 %attend.8.refs_12_ = bf16[128,512]{1,0:T(8,128)(2,1)} custom-call(s32[4]{0:T(128)} %copy-done.21, s32[4]{0:T(128)} %select_reduce_fusion.order_ref, bf16[512,1024]{1,0:T(8,128)(2,1)} %q_ref.5, bf16[64,256,128]{2,1,0:T(8,128)(2,1)} %sort_blocks.1.kv_ref), custom_call_target="tpu_custom_call" | custom-call | flops 5000000000 | bytes 4194304 | tf_op jit(solution)/shard_map/attend/pallas_call | solution.py:141
  115.8 2.7 %collective-permute-start.10 = (bf16[128,512]{1,0:T(8,128)(2,1)}, bf16[128,512]{1,0:T(8,128)(2,1)S(1)}, u32[]{:S(2)}, u32[]{:S(2)}) collective-permute-start(bf16[128,512]{1,0:T(8,128)(2,1)} %attend.8.refs_12_), channel_id=1, source_target_pairs={{0,3},{1,0},{2,1},{3,2},{4,7},{5,4},{6,5},{7,6},{8,11},{9,8},{10,9... | collective-permute-start | bytes 393224 | tf_op jit(solution)/shard_map/ppermute | solution.py:35
  118.5 1.0 collective-permute-start.11
  119.5 0.0 collective-permute-done.7.refs_9_
  119.5 0.0 collective-permute-start.12
  119.5 0.0 collective-permute-done.9.refs_11_
  119.5 10.0 %attend.9.refs_16_ = bf16[128,512]{1,0:T(8,128)(2,1)} custom-call(s32[4]{0:T(128)} %copy-done.21, s32[4]{0:T(128)} %select_reduce_fusion.order_ref, bf16[512,1024]{1,0:T(8,128)(2,1)} %q_ref.5, bf16[64,256,128]{2,1,0:T(8,128)(2,1)} %sort_blocks.1.kv_ref), custom_call_target="tpu_custom_call" | custom-call | flops 5000000000 | bytes 4194304 | tf_op jit(solution)/shard_map/attend/pallas_call | solution.py:141
  129.5 2.7 %collective-permute-start.13 = (bf16[128,512]{1,0:T(8,128)(2,1)}, bf16[128,512]{1,0:T(8,128)(2,1)S(1)}, u32[]{:S(2)}, u32[]{:S(2)}) collective-permute-start(bf16[128,512]{1,0:T(8,128)(2,1)} %attend.9.refs_16_), channel_id=1, source_target_pairs={{0,3},{1,0},{2,1},{3,2},{4,7},{5,4},{6,5},{7,6},{8,11},{9,8},{10,9... | collective-permute-start | bytes 393224 | tf_op jit(solution)/shard_map/ppermute | solution.py:35
  132.3 0.8 collective-permute-start.14
  133.0 0.0 collective-permute-done.10.refs_13_
  133.1 2.8 %collective-permute-done.13.refs_17_ = bf16[128,512]{1,0:T(8,128)(2,1)S(1)} collective-permute-done((bf16[128,512]{1,0:T(8,128)(2,1)}, bf16[128,512]{1,0:T(8,128)(2,1)S(1)}, u32[]{:S(2)}, u32[]{:S(2)}) %collective-permute-start.13) | collective-permute-done | bytes 131104 | tf_op jit(solution)/shard_map/ppermute | solution.py:35
  135.9 2.0 collective-permute-done.14.refs_18_
  137.9 1.3 collective-permute-done.15.refs_19_
  139.2 0.6 copy-done.17
  139.9 8.1 %project_partner.1 = (bf16[512,512]{1,0:T(8,128)(2,1)}, bf16[512,4096]{1,0:T(8,128)(2,1)}) custom-call(s32[4]{0:T(128)} %select_reduce_fusion.order_ref, bf16[128,1024]{1,0:T(8,128)(2,1)} %attend.5.refs_0_, bf16[128,1024]{1,0:T(8,128)(2,1)} %copy-done.3, bf16[128,1024]{1,0:T(8,128)(2,1)} %copy-done.4, bf16[128,1024]{1,0:T(8,128)(2,1)} %copy-done.5, ...), custom_call_target="tpu_custom_call" | custom-call | flops 2147483648 | bytes 14680064 | tf_op jit(solution)/shard_map/project_partner/pallas_call | solution.py:202
  147.9 6.3 %project_rest.1 = bf16[512,512]{1,0:T(8,128)(2,1)} custom-call(bf16[512,4096]{1,0:T(8,128)(2,1)} %get-tuple-element.27.a_ref, bf16[8,2,512,512]{3,2,1,0:T(8,128)(2,1)} %bitcast.6), custom_call_target="tpu_custom_call" | custom-call | flops 2147483648 | bytes 9437184 | tf_op jit(solution)/shard_map/project_rest/pallas_call | solution.py:237
  154.2 5.0 %collective-permute-start.19 = (bf16[512,512]{1,0:T(8,128)(2,1)}, bf16[512,512]{1,0:T(8,128)(2,1)S(1)}, u32[]{:S(2)}, u32[]{:S(2)}) collective-permute-start(bf16[512,512]{1,0:T(8,128)(2,1)} %project_rest.1), channel_id=1, source_target_pairs={{0,4},{4,0},{1,5},{5,1},{2,6},{6,2},{3,7},{7,3},{8,12},{12,8},{9,1... | collective-permute-start | bytes 1572872 | tf_op jit(solution)/shard_map/ppermute | solution.py:35
  159.3 0.1 collective-permute-start.18
  159.4 45.1 %all-gather.7.cloned.1.call-done = bf16[8192,512]{1,0:T(8,128)(2,1)} async-done(((bf16[512,512]{1,0:T(8,128)(2,1)}), bf16[8192,512]{1,0:T(8,128)(2,1)}) %all-gather.7.cloned.1.call-update) | async-done | bytes 8388624 | tf_op jit(solution)/shard_map/all_gather | solution.py:334
  204.4 0.8 copy-done.19
  205.2 0.2 copy-done.20
  205.4 9.4 %project_self.1 = bf16[512,1024]{1,0:T(8,128)(2,1)} custom-call(bf16[512,4096]{1,0:T(8,128)(2,1)} %get-tuple-element.27.a_ref, bf16[8,2,512,512]{3,2,1,0:T(8,128)(2,1)} %bitcast.10, bf16[512,512]{1,0:T(8,128)(2,1)} %copy-done.20, bf16[512,512]{1,0:T(8,128)(2,1)} %copy-done.19), custom_call_target="tpu_custom_call" | custom-call | flops 4294967296 | bytes 14680064 | tf_op jit(solution)/shard_map/project_self/pallas_call | solution.py:262
  (54 shorter events, 0.1 us)
Async XLA Ops:
  6.5 132.7 %all-gather.5.cloned.1.call-start = ((), (), s32[]{:S(2)}) async-start(), calls=%async_computation.1 | async-start | bytes 8912896 | tf_op jit(solution)/shard_map/all_gather | solution.py:333
  7.3 33.6 %copy-start.21 = (s32[4]{0:T(128)}, s32[4]{0:T(128)S(1)}, u32[]{:S(2)}) copy-start(s32[4]{0:T(128)S(1)} %get-tuple-element.30.own_ref) | copy-start | bytes 52
  9.0 32.9 %copy-start.1 = (bf16[1024,512]{1,0:T(8,128)(2,1)S(1)}, bf16[1024,512]{1,0:T(8,128)(2,1)}, u32[]{:S(2)}) copy-start(bf16[1024,512]{1,0:T(8,128)(2,1)} %param.9) | copy-start | bytes 3145732
  38.7 14.9 %copy-start = (bf16[8,1040,128]{2,1,0:T(8,128)(2,1)}, bf16[8,1040,128]{2,1,0:T(8,128)(2,1)S(1)}, u32[]{:S(2)}) copy-start(bf16[8,1040,128]{2,1,0:T(8,128)(2,1)S(1)} %all_to_all.5.mine_ref) | copy-start | bytes 6389764
  38.7 13.4 %collective-permute-start = (bf16[8,1040,128]{2,1,0:T(8,128)(2,1)S(1)}, bf16[8,1040,128]{2,1,0:T(8,128)(2,1)}, u32[]{:S(2)}, u32[]{:S(2)}) collective-permute-start(bf16[8,1040,128]{2,1,0:T(8,128)(2,1)S(1)} %all_to_all.5.mine_ref), channel_id=1, source_target_pairs={{0,8},{8,0},{1,9},{9,1},{2,10},{10,2},{3,11},{11,3},{4,12},{12,4},... | collective-permute-start | bytes 6389768 | tf_op jit(solution)/shard_map/ppermute | solution.py:35
  42.9 28.1 %collective-permute-start.16 = (bf16[512,512]{1,0:T(8,128)(2,1)}, bf16[512,512]{1,0:T(8,128)(2,1)S(1)}, u32[]{:S(2)}, u32[]{:S(2)}) collective-permute-start(bf16[512,512]{1,0:T(8,128)(2,1)} %get-tuple-element.34), channel_id=1, source_target_pairs={{0,16},{1,48},{2,80},{3,112},{4,4},{5,36},{6,68},{7,100},{16,113},... | collective-permute-start | bytes 1572872 | tf_op jit(solution)/shard_map/ppermute | solution.py:35
  48.4 23.0 %collective-permute-start.17 = (bf16[512,512]{1,0:T(8,128)(2,1)}, bf16[512,512]{1,0:T(8,128)(2,1)S(1)}, u32[]{:S(2)}, u32[]{:S(2)}) collective-permute-start(bf16[512,512]{1,0:T(8,128)(2,1)} %get-tuple-element.33), channel_id=1, source_target_pairs={{0,0},{1,32},{2,64},{3,96},{4,20},{5,52},{6,84},{7,116},{16,97},{1... | collective-permute-start | bytes 1572872 | tf_op jit(solution)/shard_map/ppermute | solution.py:35
  67.2 6.1 %copy-start.2 = (bf16[128,1024]{1,0:T(8,128)(2,1)S(1)}, bf16[128,1024]{1,0:T(8,128)(2,1)}, u32[]{:S(2)}) copy-start(bf16[128,1024]{1,0:T(8,128)(2,1)} %attend.5.refs_0_) | copy-start | bytes 786436
  72.5 132.0 %all-gather.7.cloned.1.call-start = ((), (), s32[]{:S(2)}) async-start(), calls=%async_computation.2 | async-start | bytes 8912896 | tf_op jit(solution)/shard_map/all_gather | solution.py:334
  73.2 17.3 %collective-permute-start.1 = (bf16[128,1024]{1,0:T(8,128)(2,1)S(1)}, bf16[128,1024]{1,0:T(8,128)(2,1)S(1)}, u32[]{:S(2)}, u32[]{:S(2)}) collective-permute-start(bf16[128,1024]{1,0:T(8,128)(2,1)S(1)} %copy-done.2), channel_id=1, source_target_pairs={{0,3},{1,0},{2,1},{3,2},{4,7},{5,4},{6,5},{7,6},{8,11},{9,8},{10,9... | collective-permute-start | bytes 786440 | tf_op jit(solution)/shard_map/ppermute | solution.py:35
  75.4 15.1 %collective-permute-start.2 = (bf16[128,1024]{1,0:T(8,128)(2,1)S(1)}, bf16[128,1024]{1,0:T(8,128)(2,1)S(1)}, u32[]{:S(2)}, u32[]{:S(2)}) collective-permute-start(bf16[128,1024]{1,0:T(8,128)(2,1)S(1)} %copy-done.2), channel_id=1, source_target_pairs={{0,2},{1,3},{2,0},{3,1},{4,6},{5,7},{6,4},{7,5},{8,10},{9,11},{10,... | collective-permute-start | bytes 786440 | tf_op jit(solution)/shard_map/ppermute | solution.py:35
  76.2 14.5 %collective-permute-start.3 = (bf16[128,1024]{1,0:T(8,128)(2,1)S(1)}, bf16[128,1024]{1,0:T(8,128)(2,1)S(1)}, u32[]{:S(2)}, u32[]{:S(2)}) collective-permute-start(bf16[128,1024]{1,0:T(8,128)(2,1)S(1)} %copy-done.2), channel_id=1, source_target_pairs={{0,1},{1,2},{2,3},{3,0},{4,5},{5,6},{6,7},{7,4},{8,9},{9,10},{10,1... | collective-permute-start | bytes 786440 | tf_op jit(solution)/shard_map/ppermute | solution.py:35
  86.8 18.7 %collective-permute-start.4 = (bf16[128,1024]{1,0:T(8,128)(2,1)}, bf16[128,1024]{1,0:T(8,128)(2,1)S(1)}, u32[]{:S(2)}, u32[]{:S(2)}) collective-permute-start(bf16[128,1024]{1,0:T(8,128)(2,1)} %attend.6.refs_4_), channel_id=1, source_target_pairs={{0,3},{1,0},{2,1},{3,2},{4,7},{5,4},{6,5},{7,6},{8,11},{9,8},{10,9... | collective-permute-start | bytes 786440 | tf_op jit(solution)/shard_map/ppermute | solution.py:35
  89.5 16.0 %collective-permute-start.5 = (bf16[128,1024]{1,0:T(8,128)(2,1)}, bf16[128,1024]{1,0:T(8,128)(2,1)S(1)}, u32[]{:S(2)}, u32[]{:S(2)}) collective-permute-start(bf16[128,1024]{1,0:T(8,128)(2,1)} %attend.6.refs_4_), channel_id=1, source_target_pairs={{0,2},{1,3},{2,0},{3,1},{4,6},{5,7},{6,4},{7,5},{8,10},{9,11},{10,... | collective-permute-start | bytes 786440 | tf_op jit(solution)/shard_map/ppermute | solution.py:35
  90.5 11.7 %copy-start.3 = (bf16[128,1024]{1,0:T(8,128)(2,1)}, bf16[128,1024]{1,0:T(8,128)(2,1)S(1)}, u32[]{:S(2)}) copy-start(bf16[128,1024]{1,0:T(8,128)(2,1)S(1)} %collective-permute-done.1.refs_1_) | copy-start | bytes 786436
  90.5 15.0 %collective-permute-start.6 = (bf16[128,1024]{1,0:T(8,128)(2,1)}, bf16[128,1024]{1,0:T(8,128)(2,1)S(1)}, u32[]{:S(2)}, u32[]{:S(2)}) collective-permute-start(bf16[128,1024]{1,0:T(8,128)(2,1)} %attend.6.refs_4_), channel_id=1, source_target_pairs={{0,1},{1,2},{2,3},{3,0},{4,5},{5,6},{6,7},{7,4},{8,9},{9,10},{10,1... | collective-permute-start | bytes 786440 | tf_op jit(solution)/shard_map/ppermute | solution.py:35
  90.5 11.7 %copy-start.4 = (bf16[128,1024]{1,0:T(8,128)(2,1)}, bf16[128,1024]{1,0:T(8,128)(2,1)S(1)}, u32[]{:S(2)}) copy-start(bf16[128,1024]{1,0:T(8,128)(2,1)S(1)} %collective-permute-done.2.refs_2_) | copy-start | bytes 786436
  90.8 11.4 %copy-start.5 = (bf16[128,1024]{1,0:T(8,128)(2,1)}, bf16[128,1024]{1,0:T(8,128)(2,1)S(1)}, u32[]{:S(2)}) copy-start(bf16[128,1024]{1,0:T(8,128)(2,1)S(1)} %collective-permute-done.3.refs_3_) | copy-start | bytes 786436
  102.2 17.3 %collective-permute-start.7 = (bf16[128,1024]{1,0:T(8,128)(2,1)}, bf16[128,1024]{1,0:T(8,128)(2,1)S(1)}, u32[]{:S(2)}, u32[]{:S(2)}) collective-permute-start(bf16[128,1024]{1,0:T(8,128)(2,1)} %attend.7.refs_8_), channel_id=1, source_target_pairs={{0,3},{1,0},{2,1},{3,2},{4,7},{5,4},{6,5},{7,6},{8,11},{9,8},{10,9... | collective-permute-start | bytes 786440 | tf_op jit(solution)/shard_map/ppermute | solution.py:35
  104.7 14.8 %collective-permute-start.8 = (bf16[128,1024]{1,0:T(8,128)(2,1)}, bf16[128,1024]{1,0:T(8,128)(2,1)S(1)}, u32[]{:S(2)}, u32[]{:S(2)}) collective-permute-start(bf16[128,1024]{1,0:T(8,128)(2,1)} %attend.7.refs_8_), channel_id=1, source_target_pairs={{0,2},{1,3},{2,0},{3,1},{4,6},{5,7},{6,4},{7,5},{8,10},{9,11},{10,... | collective-permute-start | bytes 786440 | tf_op jit(solution)/shard_map/ppermute | solution.py:35
  105.5 10.2 %copy-start.6 = (bf16[128,1024]{1,0:T(8,128)(2,1)}, bf16[128,1024]{1,0:T(8,128)(2,1)S(1)}, u32[]{:S(2)}) copy-start(bf16[128,1024]{1,0:T(8,128)(2,1)S(1)} %collective-permute-done.4.refs_5_) | copy-start | bytes 786436
  105.5 14.0 %collective-permute-start.9 = (bf16[128,1024]{1,0:T(8,128)(2,1)}, bf16[128,1024]{1,0:T(8,128)(2,1)S(1)}, u32[]{:S(2)}, u32[]{:S(2)}) collective-permute-start(bf16[128,1024]{1,0:T(8,128)(2,1)} %attend.7.refs_8_), channel_id=1, source_target_pairs={{0,1},{1,2},{2,3},{3,0},{4,5},{5,6},{6,7},{7,4},{8,9},{9,10},{10,1... | collective-permute-start | bytes 786440 | tf_op jit(solution)/shard_map/ppermute | solution.py:35
  105.5 10.2 %copy-start.7 = (bf16[128,1024]{1,0:T(8,128)(2,1)}, bf16[128,1024]{1,0:T(8,128)(2,1)S(1)}, u32[]{:S(2)}) copy-start(bf16[128,1024]{1,0:T(8,128)(2,1)S(1)} %collective-permute-done.5.refs_6_) | copy-start | bytes 786436
  105.6 10.2 %copy-start.8 = (bf16[128,1024]{1,0:T(8,128)(2,1)}, bf16[128,1024]{1,0:T(8,128)(2,1)S(1)}, u32[]{:S(2)}) copy-start(bf16[128,1024]{1,0:T(8,128)(2,1)S(1)} %collective-permute-done.6.refs_7_) | copy-start | bytes 786436
  115.8 17.3 %collective-permute-start.10 = (bf16[128,512]{1,0:T(8,128)(2,1)}, bf16[128,512]{1,0:T(8,128)(2,1)S(1)}, u32[]{:S(2)}, u32[]{:S(2)}) collective-permute-start(bf16[128,512]{1,0:T(8,128)(2,1)} %attend.8.refs_12_), channel_id=1, source_target_pairs={{0,3},{1,0},{2,1},{3,2},{4,7},{5,4},{6,5},{7,6},{8,11},{9,8},{10,9... | collective-permute-start | bytes 393224 | tf_op jit(solution)/shard_map/ppermute | solution.py:35
  118.5 14.6 %collective-permute-start.11 = (bf16[128,512]{1,0:T(8,128)(2,1)}, bf16[128,512]{1,0:T(8,128)(2,1)S(1)}, u32[]{:S(2)}, u32[]{:S(2)}) collective-permute-start(bf16[128,512]{1,0:T(8,128)(2,1)} %attend.8.refs_12_), channel_id=1, source_target_pairs={{0,2},{1,3},{2,0},{3,1},{4,6},{5,7},{6,4},{7,5},{8,10},{9,11},{10,... | collective-permute-start | bytes 393224 | tf_op jit(solution)/shard_map/ppermute | solution.py:35
  119.5 10.0 %copy-start.9 = (bf16[128,1024]{1,0:T(8,128)(2,1)}, bf16[128,1024]{1,0:T(8,128)(2,1)S(1)}, u32[]{:S(2)}) copy-start(bf16[128,1024]{1,0:T(8,128)(2,1)S(1)} %collective-permute-done.7.refs_9_) | copy-start | bytes 786436
  119.5 13.6 %collective-permute-start.12 = (bf16[128,512]{1,0:T(8,128)(2,1)}, bf16[128,512]{1,0:T(8,128)(2,1)S(1)}, u32[]{:S(2)}, u32[]{:S(2)}) collective-permute-start(bf16[128,512]{1,0:T(8,128)(2,1)} %attend.8.refs_12_), channel_id=1, source_target_pairs={{0,1},{1,2},{2,3},{3,0},{4,5},{5,6},{6,7},{7,4},{8,9},{9,10},{10,1... | collective-permute-start | bytes 393224 | tf_op jit(solution)/shard_map/ppermute | solution.py:35
  119.5 10.0 %copy-start.10 = (bf16[128,1024]{1,0:T(8,128)(2,1)}, bf16[128,1024]{1,0:T(8,128)(2,1)S(1)}, u32[]{:S(2)}) copy-start(bf16[128,1024]{1,0:T(8,128)(2,1)S(1)} %collective-permute-done.8.refs_10_) | copy-start | bytes 786436
  119.5 10.0 %copy-start.11 = (bf16[128,1024]{1,0:T(8,128)(2,1)}, bf16[128,1024]{1,0:T(8,128)(2,1)S(1)}, u32[]{:S(2)}) copy-start(bf16[128,1024]{1,0:T(8,128)(2,1)S(1)} %collective-permute-done.9.refs_11_) | copy-start | bytes 786436
  129.5 6.4 %collective-permute-start.13 = (bf16[128,512]{1,0:T(8,128)(2,1)}, bf16[128,512]{1,0:T(8,128)(2,1)S(1)}, u32[]{:S(2)}, u32[]{:S(2)}) collective-permute-start(bf16[128,512]{1,0:T(8,128)(2,1)} %attend.9.refs_16_), channel_id=1, source_target_pairs={{0,3},{1,0},{2,1},{3,2},{4,7},{5,4},{6,5},{7,6},{8,11},{9,8},{10,9... | collective-permute-start | bytes 393224 | tf_op jit(solution)/shard_map/ppermute | solution.py:35
  132.3 5.6 %collective-permute-start.14 = (bf16[128,512]{1,0:T(8,128)(2,1)}, bf16[128,512]{1,0:T(8,128)(2,1)S(1)}, u32[]{:S(2)}, u32[]{:S(2)}) collective-permute-start(bf16[128,512]{1,0:T(8,128)(2,1)} %attend.9.refs_16_), channel_id=1, source_target_pairs={{0,2},{1,3},{2,0},{3,1},{4,6},{5,7},{6,4},{7,5},{8,10},{9,11},{10,... | collective-permute-start | bytes 393224 | tf_op jit(solution)/shard_map/ppermute | solution.py:35
  133.1 6.2 %copy-start.12 = (bf16[128,512]{1,0:T(8,128)(2,1)}, bf16[128,512]{1,0:T(8,128)(2,1)S(1)}, u32[]{:S(2)}) copy-start(bf16[128,512]{1,0:T(8,128)(2,1)S(1)} %collective-permute-done.10.refs_13_) | copy-start | bytes 393220
  133.1 6.2 %collective-permute-start.15 = (bf16[128,512]{1,0:T(8,128)(2,1)}, bf16[128,512]{1,0:T(8,128)(2,1)S(1)}, u32[]{:S(2)}, u32[]{:S(2)}) collective-permute-start(bf16[128,512]{1,0:T(8,128)(2,1)} %attend.9.refs_16_), channel_id=1, source_target_pairs={{0,1},{1,2},{2,3},{3,0},{4,5},{5,6},{6,7},{7,4},{8,9},{9,10},{10,1... | collective-permute-start | bytes 393224 | tf_op jit(solution)/shard_map/ppermute | solution.py:35
  133.1 6.1 %copy-start.13 = (bf16[128,512]{1,0:T(8,128)(2,1)}, bf16[128,512]{1,0:T(8,128)(2,1)S(1)}, u32[]{:S(2)}) copy-start(bf16[128,512]{1,0:T(8,128)(2,1)S(1)} %collective-permute-done.11.refs_14_) | copy-start | bytes 393220
  133.1 6.1 %copy-start.14 = (bf16[128,512]{1,0:T(8,128)(2,1)}, bf16[128,512]{1,0:T(8,128)(2,1)S(1)}, u32[]{:S(2)}) copy-start(bf16[128,512]{1,0:T(8,128)(2,1)S(1)} %collective-permute-done.12.refs_15_) | copy-start | bytes 393220
  135.9 3.3 %copy-start.15 = (bf16[128,512]{1,0:T(8,128)(2,1)}, bf16[128,512]{1,0:T(8,128)(2,1)S(1)}, u32[]{:S(2)}) copy-start(bf16[128,512]{1,0:T(8,128)(2,1)S(1)} %collective-permute-done.13.refs_17_) | copy-start | bytes 393220
  137.9 1.3 copy-start.16
  139.2 0.7 copy-start.17
  147.9 11.4 %copy-start.18 = (bf16[512,512]{1,0:T(8,128)(2,1)S(1)}, bf16[512,512]{1,0:T(8,128)(2,1)}, u32[]{:S(2)}) copy-start(bf16[512,512]{1,0:T(8,128)(2,1)} %get-tuple-element.28) | copy-start | bytes 1572868
  154.2 50.2 %collective-permute-start.19 = (bf16[512,512]{1,0:T(8,128)(2,1)}, bf16[512,512]{1,0:T(8,128)(2,1)S(1)}, u32[]{:S(2)}, u32[]{:S(2)}) collective-permute-start(bf16[512,512]{1,0:T(8,128)(2,1)} %project_rest.1), channel_id=1, source_target_pairs={{0,4},{4,0},{1,5},{5,1},{2,6},{6,2},{3,7},{7,3},{8,12},{12,8},{9,1... | collective-permute-start | bytes 1572872 | tf_op jit(solution)/shard_map/ppermute | solution.py:35
  159.3 45.1 %collective-permute-start.18 = (bf16[512,512]{1,0:T(8,128)(2,1)S(1)}, bf16[512,512]{1,0:T(8,128)(2,1)S(1)}, u32[]{:S(2)}, u32[]{:S(2)}) collective-permute-start(bf16[512,512]{1,0:T(8,128)(2,1)S(1)} %copy-done.18), channel_id=1, source_target_pairs={{0,4},{4,0},{1,5},{5,1},{2,6},{6,2},{3,7},{7,3},{8,12},{12,8},{9,1... | collective-permute-start | bytes 1572872 | tf_op jit(solution)/shard_map/ppermute | solution.py:35
  204.4 0.8 copy-start.19
  204.4 1.0 copy-start.20
Sparse Core Ops, SparseCore 0:
  72.6 57.5 all-gather.4
  131.9 72.4 all-gather.6

commit v2 on v0

--- a/solution.py
+++ b/solution.py
@@ -209,7 +209,7 @@
             num_scalar_prefetch=1,
             grid=(2,),
             in_specs=[pl.BlockSpec(memory_space=pl.ANY)] * len(pieces)
-            + [pl.BlockSpec((8, None, 512, 256), lambda n, o: (0, 0, 0, n))],
+            + [pl.BlockSpec((8, None, None, 512, 256), lambda n, o: (0, 0, 0, 0, n))],
             out_specs=(
                 pl.BlockSpec((512, 256), lambda n, o: (0, n)),
                 pl.BlockSpec(memory_space=pl.ANY),
@@ -240,7 +240,7 @@
         grid=(2,),
         in_specs=[
             pl.BlockSpec((512, 4096), lambda n: (0, 0)),
-            pl.BlockSpec((8, None, 512, 256), lambda n: (0, 1, 0, n)),
+            pl.BlockSpec((8, None, None, 512, 256), lambda n: (0, 1, 0, 0, n)),
         ],
         out_specs=pl.BlockSpec((512, 256), lambda n: (0, n)),
         compiler_params=pltpu.CompilerParams(vmem_limit_bytes=VMEM_BYTES),
@@ -251,23 +251,19 @@
     )(rows, weight)
 
 
-def project_self(a_ref, w_ref, first_ref, second_ref, out_ref):
+def project_self(a_ref, w_ref, out_ref):
     w = w_ref[...].reshape(4096, 256)
-    out = jnp.dot(a_ref[...], w, preferred_element_type=jnp.float32)
-    other = jnp.where(pl.program_id(0) < 2, first_ref[...], second_ref[...])
-    out_ref[...] = (out + other.astype(jnp.float32)).astype(jnp.bfloat16)
-
-
-def own_terms(rows, weight, first, second):
+    out_ref[...] = jnp.dot(a_ref[...], w, preferred_element_type=jnp.float32)
+
+
+def own_terms(rows, weight):
     return pl.pallas_call(
         project_self,
-        out_shape=jax.ShapeDtypeStruct((512, 1024), jnp.bfloat16),
+        out_shape=jax.ShapeDtypeStruct((512, 1024), jnp.float32),
         grid=(4,),
         in_specs=[
             pl.BlockSpec((512, 4096), lambda n: (0, 0)),
-            pl.BlockSpec((8, None, 512, 256), lambda n: (0, n // 2, 0, n % 2)),
-            pl.BlockSpec((512, 256), lambda n: (0, jnp.minimum(n, 1))),
-            pl.BlockSpec((512, 256), lambda n: (0, jnp.maximum(n - 2, 0))),
+            pl.BlockSpec((8, None, None, 512, 256), lambda n: (0, n // 2, 1, 0, n % 2)),
         ],
         out_specs=pl.BlockSpec((512, 256), lambda n: (0, n)),
         compiler_params=pltpu.CompilerParams(vmem_limit_bytes=VMEM_BYTES),
@@ -275,7 +271,7 @@
             flops=2 * 512 * 4096 * 1024, bytes_accessed=14 << 20, transcendentals=0
         ),
         name="project_self",
-    )(rows, weight, first, second)
+    )(rows, weight)
 
 
 def spread_target(half):
@@ -314,14 +310,12 @@
     got_first = move(first, plane, spread_target(0))
     got_second = move(second, plane, spread_target(1))
     got_first, got_second, mine = lax.optimization_barrier((got_first, got_second, mine))
-    for_partner = jnp.where(xl == 0, got_first, got_second)
-    for_self = jnp.where(xl == 0, got_second, got_first)
-    weight_partner = lax.all_gather(for_partner, ("y", "xl", "c")).reshape(8, 2, 512, 512)
-    weight_self = lax.all_gather(for_self, ("y", "xl", "c")).reshape(8, 2, 512, 512)
-
     theirs = swap_cores(mine)
+    both = jnp.where(xl == 0, jnp.stack([got_first, got_second]), jnp.stack([got_second, got_first]))
+    weight = lax.all_gather(both.reshape(1024, 512), ("y", "xl", "c")).reshape(8, 2, 2, 512, 512)
     slots = jnp.concatenate([mine[:, 1024:1028, 0].reshape(32), theirs[:, 1024:1028, 0].reshape(32)])
     kv = sorted_kv(slots.astype(jnp.int32), mine, theirs)
+
     sets, places = [], []
     for chunk, part, heads in ((0, 0, 8), (1, 0, 8), (2, 0, 8), (3, 0, 4), (3, 1, 4)):
         if sets:
@@ -333,11 +327,13 @@
         sets.append([piece] + around)
         places += [(chunk, dz * 1024 + part * 512) for dz in range(4)]
     pieces = [piece for group in sets for piece in group]
-    first_sum, rows = partner_terms(order, pieces, tuple(places), weight_partner)
+    first_sum, rows = partner_terms(order, pieces, tuple(places), weight)
     got_first = move(first_sum, ("xh",), lambda a: (a + 1,))
-    second_sum = rest_terms(rows, weight_partner)
+    second_sum = rest_terms(rows, weight)
     got_second = move(second_sum, ("xh",), lambda a: (a + 1,))
-    return own_terms(rows, weight_self, got_first, got_second)
+    own_sum = own_terms(rows, weight)
+    others = jnp.concatenate([got_first, got_second], axis=1)
+    return (own_sum + others.astype(jnp.float32)).astype(jnp.bfloat16)
 
 
 def solution(mesh):

time: 217 us -> 214 us (0.986)
  Pallas kernels: 83.7 us -> 65.4 us
  waiting for transfers between devices: 72.1 us -> 81.7 us
  starting transfers between devices: 36.1 us -> 39.3 us
  other arithmetic: 3.96 us -> 6.87 us
    pallas_call x5, Pallas kernels: 54.5 us -> 36.3 us  [attention(): pl.pallas_call(functools.partial(attend, chunk, heads), out_shape=jax.Sha...]
    all_gather x2 -> x1, waiting for transfers between devices: 3.05 us -> 20.8 us  [per_device(): lax.all_gather(both.reshape(1024, 512), ('y', 'xl', 'c'))]
    ppermute x20, waiting for transfers between devices: 68.3 us -> 60.8 us  [move(): return lax.ppermute(block, axes, route)]
    ppermute x20, starting transfers between devices: 30.9 us -> 34.1 us  [move(): return lax.ppermute(block, axes, route)]
    convert_element_type x0 -> x1, other arithmetic: none -> 2.89 us  [per_device(): return (own_sum + others.astype(jnp.float32)).astype(jnp.bfloat16)]
  transfers between devices with their start and end apart: 23 -> 22, of which waited for: 8 -> 10; matrix products, arithmetic and copies ran while one was open for 2% -> 2% of each run, Pallas kernels for 34% -> 24%
where the time goes in v2:
time: 214 us; the launch traced here: 212 us
  waiting for transfers between devices  81.7 us (38%)
  Pallas kernels  65.4 us (31%)
  starting transfers between devices  39.3 us (18%)
  between operations  13.7 us (6%)
  other arithmetic  6.87 us (3%)
  local copies, waits for them, and re-layouts  4.72 us (2%)
    ppermute x20, waiting for transfers between devices, move(): return lax.ppermute(block, axes, route)  60.8 us
    pallas_call x5, Pallas kernels, attention(): pl.pallas_call(functools.partial(attend, chunk, heads), out_shape=jax.Sha...  36.3 us
    ppermute x20, starting transfers between devices, move(): return lax.ppermute(block, axes, route)  34.1 us
    all_gather x1, waiting for transfers between devices, per_device(): lax.all_gather(both.reshape(1024, 512), ('y', 'xl', 'c'))  20.8 us
    pallas_call x1, Pallas kernels, own_terms(): pl.pallas_call(project_self, out_shape=jax.ShapeDtypeStruct((512, 1024),...  9.45 us
    pallas_call x1, Pallas kernels, partner_terms(): pl.pallas_call(functools.partial(project_partner, places), out_shape=(jax...  8.07 us
    pallas_call x1, Pallas kernels, rest_terms(): pl.pallas_call(project_rest, out_shape=jax.ShapeDtypeStruct((512, 512), j...  6.16 us
    pallas_call x1, Pallas kernels, sorted_kv(): pl.pallas_call(sort_blocks, out_shape=jax.ShapeDtypeStruct((64, 2 * BLK,...  5.39 us
  transfers between devices with their start and end apart: 22, of which 10 were waited for; matrix products, arithmetic and copies ran while one was open for 2% of the time, Pallas kernels for 24%

profile of v2, /device:TPU:25, one launch (start us, length us, event | category | flops | bytes accessed | tf_op | source)
XLA Modules:
  0.0 211.6 jit_solution(12799715178229522227)
XLA Ops:
  6.5 0.8 slice.9
  7.3 0.1 reshape.36
  7.4 1.0 pad_maximum_fusion.1
  8.5 0.2 pad_maximum_fusion
  8.7 1.6 broadcast_in_dim.38
  10.3 5.2 %all-to-all-start = ((bf16[8,1040,128]{2,1,0:T(8,128)(2,1)}), bf16[8,1040,128]{2,1,0:T(8,128)(2,1)S(1)}, u32[]{:S(2)}, u32[]{:S(2)}) async-start(bf16[8,1040,128]{2,1,0:T(8,128)(2,1)} %broadcast_in_dim.38), calls=%async_computation | async-start | bytes 4259840 | tf_op jit(solution)/shard_map/all_to_all | solution.py:301
  15.5 1.0 constant_dynamic-slice_fusion
  16.6 6.7 %collective-permute-start.1 = (bf16[512,512]{1,0:T(8,128)(2,1)}, bf16[512,512]{1,0:T(8,128)(2,1)S(1)}, u32[]{:S(2)}, u32[]{:S(2)}) collective-permute-start(bf16[512,512]{1,0:T(8,128)(2,1)} %get-tuple-element.31), channel_id=1, source_target_pairs={{0,0},{1,32},{2,64},{3,96},{4,20},{5,52},{6,84},{7,116},{16,97},{1... | collective-permute-start | bytes 1572872 | tf_op jit(solution)/shard_map/ppermute | solution.py:35
  23.2 1.9 collective-permute-start
  25.2 33.2 %collective-permute-done.1 = bf16[512,512]{1,0:T(8,128)(2,1)S(1)} collective-permute-done((bf16[512,512]{1,0:T(8,128)(2,1)}, bf16[512,512]{1,0:T(8,128)(2,1)S(1)}, u32[]{:S(2)}, u32[]{:S(2)}) %collective-permute-start.1) | collective-permute-done | bytes 524320 | tf_op jit(solution)/shard_map/ppermute | solution.py:35
  58.4 3.7 %collective-permute-done = bf16[512,512]{1,0:T(8,128)(2,1)S(1)} collective-permute-done((bf16[512,512]{1,0:T(8,128)(2,1)}, bf16[512,512]{1,0:T(8,128)(2,1)S(1)}, u32[]{:S(2)}, u32[]{:S(2)}) %collective-permute-start) | collective-permute-done | bytes 524320 | tf_op jit(solution)/shard_map/ppermute | solution.py:35
  62.1 0.0 all-to-all-done.mine_ref
  62.1 1.3 maximum_select_fusion
  63.4 0.0 all-gather.2.cloned.1.call-update
  63.4 2.0 collective-permute-start.2
  65.4 0.2 convert_reduce_fusion
  65.6 0.6 select_reduce_fusion.order_ref
  66.2 0.1 slice_reduce_fusion.1
  66.3 0.1 reshape_squeeze.6
  66.4 3.0 %collective-permute-done.2.other_ref = bf16[8,1040,128]{2,1,0:T(8,128)(2,1)} collective-permute-done((bf16[8,1040,128]{2,1,0:T(8,128)(2,1)S(1)}, bf16[8,1040,128]{2,1,0:T(8,128)(2,1)}, u32[]{:S(2)}, u32[]{:S(2)}) %collective-permute-start.2) | collective-permute-done | bytes 2129952 | tf_op jit(solution)/shard_map/ppermute | solution.py:35
  69.4 0.8 slice_reduce_fusion
  70.2 0.1 reshape_squeeze.7
  70.3 0.7 maximum_convert_fusion.slot_ref
  71.0 5.4 %sort_blocks.1.kv_ref = bf16[64,256,128]{2,1,0:T(8,128)(2,1)} custom-call(s32[64]{0:T(128)} %maximum_convert_fusion.slot_ref, bf16[8,1040,128]{2,1,0:T(8,128)(2,1)} %copy-done, bf16[8,1040,128]{2,1,0:T(8,128)(2,1)} %collective-permute-done.2.other_ref), custom_call_target="tpu_custom_call" | custom-call | bytes 8388608 | tf_op jit(solution)/shard_map/sort_blocks/pallas_call | solution.py:60
  76.4 4.7 %attend.5.refs_0_ = bf16[128,1024]{1,0:T(8,128)(2,1)} custom-call(s32[4]{0:T(128)} %copy-done.18, s32[4]{0:T(128)} %select_reduce_fusion.order_ref, bf16[512,1024]{1,0:T(8,128)(2,1)} %q_ref.5, bf16[64,256,128]{2,1,0:T(8,128)(2,1)} %sort_blocks.1.kv_ref), custom_call_target="tpu_custom_call" | custom-call | flops 10000000000 | bytes 4194304 | tf_op jit(solution)/shard_map/attend/pallas_call | solution.py:141
  81.1 0.7 collective-permute-start.5
  81.8 3.5 %collective-permute-start.4 = (bf16[128,1024]{1,0:T(8,128)(2,1)}, bf16[128,1024]{1,0:T(8,128)(2,1)S(1)}, u32[]{:S(2)}, u32[]{:S(2)}) collective-permute-start(bf16[128,1024]{1,0:T(8,128)(2,1)} %attend.5.refs_0_), channel_id=1, source_target_pairs={{0,2},{1,3},{2,0},{3,1},{4,6},{5,7},{6,4},{7,5},{8,10},{9,11},{10,... | collective-permute-start | bytes 786440 | tf_op jit(solution)/shard_map/ppermute | solution.py:35
  85.3 0.0 collective-permute-start.3
  85.3 5.6 %attend.6.refs_4_ = bf16[128,1024]{1,0:T(8,128)(2,1)} custom-call(s32[4]{0:T(128)} %copy-done.18, s32[4]{0:T(128)} %select_reduce_fusion.order_ref, bf16[512,1024]{1,0:T(8,128)(2,1)} %q_ref.5, bf16[64,256,128]{2,1,0:T(8,128)(2,1)} %sort_blocks.1.kv_ref), custom_call_target="tpu_custom_call" | custom-call | flops 10000000000 | bytes 4194304 | tf_op jit(solution)/shard_map/attend/pallas_call | solution.py:141
  90.9 1.5 collective-permute-start.8
  92.4 0.0 collective-permute-start.7
  92.5 0.0 collective-permute-done.5.refs_3_
  92.5 2.4 %collective-permute-start.6 = (bf16[128,1024]{1,0:T(8,128)(2,1)}, bf16[128,1024]{1,0:T(8,128)(2,1)S(1)}, u32[]{:S(2)}, u32[]{:S(2)}) collective-permute-start(bf16[128,1024]{1,0:T(8,128)(2,1)} %attend.6.refs_4_), channel_id=1, source_target_pairs={{0,3},{1,0},{2,1},{3,2},{4,7},{5,4},{6,5},{7,6},{8,11},{9,8},{10,9... | collective-permute-start | bytes 786440 | tf_op jit(solution)/shard_map/ppermute | solution.py:35
  94.9 1.3 collective-permute-done.4.refs_2_
  96.2 1.4 collective-permute-done.3.refs_1_
  97.6 8.9 %attend.7.refs_8_ = bf16[128,1024]{1,0:T(8,128)(2,1)} custom-call(s32[4]{0:T(128)} %copy-done.18, s32[4]{0:T(128)} %select_reduce_fusion.order_ref, bf16[512,1024]{1,0:T(8,128)(2,1)} %q_ref.5, bf16[64,256,128]{2,1,0:T(8,128)(2,1)} %sort_blocks.1.kv_ref), custom_call_target="tpu_custom_call" | custom-call | flops 10000000000 | bytes 4194304 | tf_op jit(solution)/shard_map/attend/pallas_call | solution.py:141
  106.6 0.5 collective-permute-start.11
  107.0 4.6 %collective-permute-start.10 = (bf16[128,1024]{1,0:T(8,128)(2,1)}, bf16[128,1024]{1,0:T(8,128)(2,1)S(1)}, u32[]{:S(2)}, u32[]{:S(2)}) collective-permute-start(bf16[128,1024]{1,0:T(8,128)(2,1)} %attend.7.refs_8_), channel_id=1, source_target_pairs={{0,2},{1,3},{2,0},{3,1},{4,6},{5,7},{6,4},{7,5},{8,10},{9,11},{10,... | collective-permute-start | bytes 786440 | tf_op jit(solution)/shard_map/ppermute | solution.py:35
  111.6 0.0 collective-permute-done.7.refs_6_
  111.7 8.6 %attend.8.refs_12_ = bf16[128,512]{1,0:T(8,128)(2,1)} custom-call(s32[4]{0:T(128)} %copy-done.18, s32[4]{0:T(128)} %select_reduce_fusion.order_ref, bf16[512,1024]{1,0:T(8,128)(2,1)} %q_ref.5, bf16[64,256,128]{2,1,0:T(8,128)(2,1)} %sort_blocks.1.kv_ref), custom_call_target="tpu_custom_call" | custom-call | flops 5000000000 | bytes 4194304 | tf_op jit(solution)/shard_map/attend/pallas_call | solution.py:141
  120.3 1.5 collective-permute-start.14
  121.8 0.1 collective-permute-start.13
  121.9 2.4 %collective-permute-start.12 = (bf16[128,512]{1,0:T(8,128)(2,1)}, bf16[128,512]{1,0:T(8,128)(2,1)S(1)}, u32[]{:S(2)}, u32[]{:S(2)}) collective-permute-start(bf16[128,512]{1,0:T(8,128)(2,1)} %attend.8.refs_12_), channel_id=1, source_target_pairs={{0,3},{1,0},{2,1},{3,2},{4,7},{5,4},{6,5},{7,6},{8,11},{9,8},{10,9... | collective-permute-start | bytes 393224 | tf_op jit(solution)/shard_map/ppermute | solution.py:35
  124.3 0.0 collective-permute-done.10.refs_10_
  124.3 0.0 collective-permute-done.9.refs_9_
  124.3 8.5 %attend.9.refs_16_ = bf16[128,512]{1,0:T(8,128)(2,1)} custom-call(s32[4]{0:T(128)} %copy-done.18, s32[4]{0:T(128)} %select_reduce_fusion.order_ref, bf16[512,1024]{1,0:T(8,128)(2,1)} %q_ref.5, bf16[64,256,128]{2,1,0:T(8,128)(2,1)} %sort_blocks.1.kv_ref), custom_call_target="tpu_custom_call" | custom-call | flops 5000000000 | bytes 4194304 | tf_op jit(solution)/shard_map/attend/pallas_call | solution.py:141
  132.9 0.1 collective-permute-start.17
  133.0 1.9 collective-permute-start.16
  134.9 0.0 collective-permute-done.14.refs_15_
  134.9 1.2 collective-permute-start.15
  136.1 0.0 collective-permute-done.13.refs_14_
  136.1 3.5 %collective-permute-done.17.refs_19_ = bf16[128,512]{1,0:T(8,128)(2,1)S(1)} collective-permute-done((bf16[128,512]{1,0:T(8,128)(2,1)}, bf16[128,512]{1,0:T(8,128)(2,1)S(1)}, u32[]{:S(2)}, u32[]{:S(2)}) %collective-permute-start.17) | collective-permute-done | bytes 131104 | tf_op jit(solution)/shard_map/ppermute | solution.py:35
  139.6 0.0 collective-permute-done.16.refs_18_
  139.6 1.0 collective-permute-done.15.refs_17_
  140.6 20.8 %all-gather.2.cloned.1.call-done = bf16[16,1024,512]{2,1,0:T(8,128)(2,1)} async-done(((bf16[1,1024,512]{2,1,0:T(8,128)(2,1)}), bf16[16,1024,512]{2,1,0:T(8,128)(2,1)}) %all-gather.2.cloned.1.call-update) | async-done | bytes 16777232 | tf_op jit(solution)/shard_map/all_gather | solution.py:315
  161.4 8.1 %project_partner.1 = (bf16[512,512]{1,0:T(8,128)(2,1)}, bf16[512,4096]{1,0:T(8,128)(2,1)}) custom-call(s32[4]{0:T(128)} %select_reduce_fusion.order_ref, bf16[128,1024]{1,0:T(8,128)(2,1)} %attend.5.refs_0_, bf16[128,1024]{1,0:T(8,128)(2,1)} %copy-done.4, bf16[128,1024]{1,0:T(8,128)(2,1)} %copy-done.3, bf16[128,1024]{1,0:T(8,128)(2,1)} %copy-done.2, ...), custom_call_target="tpu_custom_call" | custom-call | flops 2147483648 | bytes 14680064 | tf_op jit(solution)/shard_map/project_partner/pallas_call | solution.py:202
  169.5 0.0 copy-start.17
  169.5 6.2 %project_rest.1 = bf16[512,512]{1,0:T(8,128)(2,1)} custom-call(bf16[512,4096]{1,0:T(8,128)(2,1)} %get-tuple-element.27.a_ref, bf16[8,2,2,512,512]{4,3,2,1,0:T(8,128)(2,1)} %bitcast.8), custom_call_target="tpu_custom_call" | custom-call | flops 2147483648 | bytes 9437184 | tf_op jit(solution)/shard_map/project_rest/pallas_call | solution.py:237
  175.7 2.4 %collective-permute-start.19 = (bf16[512,512]{1,0:T(8,128)(2,1)}, bf16[512,512]{1,0:T(8,128)(2,1)S(1)}, u32[]{:S(2)}, u32[]{:S(2)}) collective-permute-start(bf16[512,512]{1,0:T(8,128)(2,1)} %project_rest.1), channel_id=1, source_target_pairs={{0,4},{4,0},{1,5},{5,1},{2,6},{6,2},{3,7},{7,3},{8,12},{12,8},{9,1... | collective-permute-start | bytes 1572872 | tf_op jit(solution)/shard_map/ppermute | solution.py:35
  178.1 0.6 collective-permute-start.18
  178.6 9.4 %project_self.1 = f32[512,1024]{1,0:T(8,128)} custom-call(bf16[512,4096]{1,0:T(8,128)(2,1)} %get-tuple-element.27.a_ref, bf16[8,2,2,512,512]{4,3,2,1,0:T(8,128)(2,1)} %bitcast.9), custom_call_target="tpu_custom_call" | custom-call | flops 4294967296 | bytes 14680064 | tf_op jit(solution)/shard_map/project_self/pallas_call | solution.py:260
  188.1 2.6 %collective-permute-done.19 = bf16[512,512]{1,0:T(8,128)(2,1)S(1)} collective-permute-done((bf16[512,512]{1,0:T(8,128)(2,1)}, bf16[512,512]{1,0:T(8,128)(2,1)S(1)}, u32[]{:S(2)}, u32[]{:S(2)}) %collective-permute-start.19) | collective-permute-done | bytes 524320 | tf_op jit(solution)/shard_map/ppermute | solution.py:35
  190.6 11.2 %collective-permute-done.18 = bf16[512,512]{1,0:T(8,128)(2,1)S(1)} collective-permute-done((bf16[512,512]{1,0:T(8,128)(2,1)S(1)}, bf16[512,512]{1,0:T(8,128)(2,1)S(1)}, u32[]{:S(2)}, u32[]{:S(2)}) %collective-permute-start.18) | collective-permute-done | bytes 524320 | tf_op jit(solution)/shard_map/ppermute | solution.py:35
  201.9 2.9 %add_convert_fusion = bf16[512,1024]{1,0:T(8,128)(2,1)} fusion(f32[512,1024]{1,0:T(8,128)} %project_self.1, bf16[512,512]{1,0:T(8,128)(2,1)S(1)} %collective-permute-done.19, bf16[512,512]{1,0:T(8,128)(2,1)S(1)} %collective-permute-done.18), kind=kLoop, calls=%fused_computation | loop fusion | flops 3145728 | bytes 4194304 | tf_op jit(solution)/shard_map/convert_element_type | solution.py:336
  (47 shorter events, 0.1 us)
Async XLA Ops:
  7.3 58.1 %copy-start.18 = (s32[4]{0:T(128)}, s32[4]{0:T(128)S(1)}, u32[]{:S(2)}) copy-start(s32[4]{0:T(128)S(1)} %get-tuple-element.30.own_ref) | copy-start | bytes 52
  10.3 5.2 %copy-start.1 = (bf16[1024,512]{1,0:T(8,128)(2,1)S(1)}, bf16[1024,512]{1,0:T(8,128)(2,1)}, u32[]{:S(2)}) copy-start(bf16[1024,512]{1,0:T(8,128)(2,1)} %param.9) | copy-start | bytes 3145732
  10.3 51.8 %all-to-all-start = ((bf16[8,1040,128]{2,1,0:T(8,128)(2,1)}), bf16[8,1040,128]{2,1,0:T(8,128)(2,1)S(1)}, u32[]{:S(2)}, u32[]{:S(2)}) async-start(bf16[8,1040,128]{2,1,0:T(8,128)(2,1)} %broadcast_in_dim.38), calls=%async_computation | async-start | bytes 4259840 | tf_op jit(solution)/shard_map/all_to_all | solution.py:301
  15.5 145.9 %all-gather.2.cloned.1.call-start = ((), (), s32[]{:S(2)}) async-start(), calls=%async_computation.1 | async-start | bytes 17825792 | tf_op jit(solution)/shard_map/all_gather | solution.py:315
  16.6 41.8 %collective-permute-start.1 = (bf16[512,512]{1,0:T(8,128)(2,1)}, bf16[512,512]{1,0:T(8,128)(2,1)S(1)}, u32[]{:S(2)}, u32[]{:S(2)}) collective-permute-start(bf16[512,512]{1,0:T(8,128)(2,1)} %get-tuple-element.31), channel_id=1, source_target_pairs={{0,0},{1,32},{2,64},{3,96},{4,20},{5,52},{6,84},{7,116},{16,97},{1... | collective-permute-start | bytes 1572872 | tf_op jit(solution)/shard_map/ppermute | solution.py:35
  23.2 38.8 %collective-permute-start = (bf16[512,512]{1,0:T(8,128)(2,1)}, bf16[512,512]{1,0:T(8,128)(2,1)S(1)}, u32[]{:S(2)}, u32[]{:S(2)}) collective-permute-start(bf16[512,512]{1,0:T(8,128)(2,1)} %get-tuple-element.32), channel_id=1, source_target_pairs={{0,16},{1,48},{2,80},{3,112},{4,4},{5,36},{6,68},{7,100},{16,113},... | collective-permute-start | bytes 1572872 | tf_op jit(solution)/shard_map/ppermute | solution.py:35
  62.1 8.9 %copy-start = (bf16[8,1040,128]{2,1,0:T(8,128)(2,1)}, bf16[8,1040,128]{2,1,0:T(8,128)(2,1)S(1)}, u32[]{:S(2)}) copy-start(bf16[8,1040,128]{2,1,0:T(8,128)(2,1)S(1)} %all-to-all-done.mine_ref) | copy-start | bytes 6389764
  63.4 6.0 %collective-permute-start.2 = (bf16[8,1040,128]{2,1,0:T(8,128)(2,1)S(1)}, bf16[8,1040,128]{2,1,0:T(8,128)(2,1)}, u32[]{:S(2)}, u32[]{:S(2)}) collective-permute-start(bf16[8,1040,128]{2,1,0:T(8,128)(2,1)S(1)} %all-to-all-done.mine_ref), channel_id=1, source_target_pairs={{0,8},{8,0},{1,9},{9,1},{2,10},{10,2},{3,11},{11,3},{4,12},{12,4},... | collective-permute-start | bytes 6389768 | tf_op jit(solution)/shard_map/ppermute | solution.py:35
  81.1 11.4 %collective-permute-start.5 = (bf16[128,1024]{1,0:T(8,128)(2,1)}, bf16[128,1024]{1,0:T(8,128)(2,1)S(1)}, u32[]{:S(2)}, u32[]{:S(2)}) collective-permute-start(bf16[128,1024]{1,0:T(8,128)(2,1)} %attend.5.refs_0_), channel_id=1, source_target_pairs={{0,1},{1,2},{2,3},{3,0},{4,5},{5,6},{6,7},{7,4},{8,9},{9,10},{10,1... | collective-permute-start | bytes 786440 | tf_op jit(solution)/shard_map/ppermute | solution.py:35
  81.8 14.4 %collective-permute-start.4 = (bf16[128,1024]{1,0:T(8,128)(2,1)}, bf16[128,1024]{1,0:T(8,128)(2,1)S(1)}, u32[]{:S(2)}, u32[]{:S(2)}) collective-permute-start(bf16[128,1024]{1,0:T(8,128)(2,1)} %attend.5.refs_0_), channel_id=1, source_target_pairs={{0,2},{1,3},{2,0},{3,1},{4,6},{5,7},{6,4},{7,5},{8,10},{9,11},{10,... | collective-permute-start | bytes 786440 | tf_op jit(solution)/shard_map/ppermute | solution.py:35
  85.3 12.3 %collective-permute-start.3 = (bf16[128,1024]{1,0:T(8,128)(2,1)}, bf16[128,1024]{1,0:T(8,128)(2,1)S(1)}, u32[]{:S(2)}, u32[]{:S(2)}) collective-permute-start(bf16[128,1024]{1,0:T(8,128)(2,1)} %attend.5.refs_0_), channel_id=1, source_target_pairs={{0,3},{1,0},{2,1},{3,2},{4,7},{5,4},{6,5},{7,6},{8,11},{9,8},{10,9... | collective-permute-start | bytes 786440 | tf_op jit(solution)/shard_map/ppermute | solution.py:35
  90.9 20.7 %collective-permute-start.8 = (bf16[128,1024]{1,0:T(8,128)(2,1)}, bf16[128,1024]{1,0:T(8,128)(2,1)S(1)}, u32[]{:S(2)}, u32[]{:S(2)}) collective-permute-start(bf16[128,1024]{1,0:T(8,128)(2,1)} %attend.6.refs_4_), channel_id=1, source_target_pairs={{0,1},{1,2},{2,3},{3,0},{4,5},{5,6},{6,7},{7,4},{8,9},{9,10},{10,1... | collective-permute-start | bytes 786440 | tf_op jit(solution)/shard_map/ppermute | solution.py:35
  92.4 19.2 %collective-permute-start.7 = (bf16[128,1024]{1,0:T(8,128)(2,1)}, bf16[128,1024]{1,0:T(8,128)(2,1)S(1)}, u32[]{:S(2)}, u32[]{:S(2)}) collective-permute-start(bf16[128,1024]{1,0:T(8,128)(2,1)} %attend.6.refs_4_), channel_id=1, source_target_pairs={{0,2},{1,3},{2,0},{3,1},{4,6},{5,7},{6,4},{7,5},{8,10},{9,11},{10,... | collective-permute-start | bytes 786440 | tf_op jit(solution)/shard_map/ppermute | solution.py:35
  92.5 14.0 %copy-start.2 = (bf16[128,1024]{1,0:T(8,128)(2,1)}, bf16[128,1024]{1,0:T(8,128)(2,1)S(1)}, u32[]{:S(2)}) copy-start(bf16[128,1024]{1,0:T(8,128)(2,1)S(1)} %collective-permute-done.5.refs_3_) | copy-start | bytes 786436
  92.5 19.2 %collective-permute-start.6 = (bf16[128,1024]{1,0:T(8,128)(2,1)}, bf16[128,1024]{1,0:T(8,128)(2,1)S(1)}, u32[]{:S(2)}, u32[]{:S(2)}) collective-permute-start(bf16[128,1024]{1,0:T(8,128)(2,1)} %attend.6.refs_4_), channel_id=1, source_target_pairs={{0,3},{1,0},{2,1},{3,2},{4,7},{5,4},{6,5},{7,6},{8,11},{9,8},{10,9... | collective-permute-start | bytes 786440 | tf_op jit(solution)/shard_map/ppermute | solution.py:35
  96.2 10.3 %copy-start.3 = (bf16[128,1024]{1,0:T(8,128)(2,1)}, bf16[128,1024]{1,0:T(8,128)(2,1)S(1)}, u32[]{:S(2)}) copy-start(bf16[128,1024]{1,0:T(8,128)(2,1)S(1)} %collective-permute-done.4.refs_2_) | copy-start | bytes 786436
  97.6 8.9 %copy-start.4 = (bf16[128,1024]{1,0:T(8,128)(2,1)}, bf16[128,1024]{1,0:T(8,128)(2,1)S(1)}, u32[]{:S(2)}) copy-start(bf16[128,1024]{1,0:T(8,128)(2,1)S(1)} %collective-permute-done.3.refs_1_) | copy-start | bytes 786436
  106.6 15.3 %collective-permute-start.11 = (bf16[128,1024]{1,0:T(8,128)(2,1)}, bf16[128,1024]{1,0:T(8,128)(2,1)S(1)}, u32[]{:S(2)}, u32[]{:S(2)}) collective-permute-start(bf16[128,1024]{1,0:T(8,128)(2,1)} %attend.7.refs_8_), channel_id=1, source_target_pairs={{0,1},{1,2},{2,3},{3,0},{4,5},{5,6},{6,7},{7,4},{8,9},{9,10},{10,1... | collective-permute-start | bytes 786440 | tf_op jit(solution)/shard_map/ppermute | solution.py:35
  107.0 17.3 %collective-permute-start.10 = (bf16[128,1024]{1,0:T(8,128)(2,1)}, bf16[128,1024]{1,0:T(8,128)(2,1)S(1)}, u32[]{:S(2)}, u32[]{:S(2)}) collective-permute-start(bf16[128,1024]{1,0:T(8,128)(2,1)} %attend.7.refs_8_), channel_id=1, source_target_pairs={{0,2},{1,3},{2,0},{3,1},{4,6},{5,7},{6,4},{7,5},{8,10},{9,11},{10,... | collective-permute-start | bytes 786440 | tf_op jit(solution)/shard_map/ppermute | solution.py:35
  111.6 8.7 %copy-start.5 = (bf16[128,1024]{1,0:T(8,128)(2,1)}, bf16[128,1024]{1,0:T(8,128)(2,1)S(1)}, u32[]{:S(2)}) copy-start(bf16[128,1024]{1,0:T(8,128)(2,1)S(1)} %collective-permute-done.8.refs_7_) | copy-start | bytes 786436
  111.6 12.7 %collective-permute-start.9 = (bf16[128,1024]{1,0:T(8,128)(2,1)}, bf16[128,1024]{1,0:T(8,128)(2,1)S(1)}, u32[]{:S(2)}, u32[]{:S(2)}) collective-permute-start(bf16[128,1024]{1,0:T(8,128)(2,1)} %attend.7.refs_8_), channel_id=1, source_target_pairs={{0,3},{1,0},{2,1},{3,2},{4,7},{5,4},{6,5},{7,6},{8,11},{9,8},{10,9... | collective-permute-start | bytes 786440 | tf_op jit(solution)/shard_map/ppermute | solution.py:35
  111.6 8.7 %copy-start.6 = (bf16[128,1024]{1,0:T(8,128)(2,1)}, bf16[128,1024]{1,0:T(8,128)(2,1)S(1)}, u32[]{:S(2)}) copy-start(bf16[128,1024]{1,0:T(8,128)(2,1)S(1)} %collective-permute-done.7.refs_6_) | copy-start | bytes 786436
  111.6 8.7 %copy-start.7 = (bf16[128,1024]{1,0:T(8,128)(2,1)}, bf16[128,1024]{1,0:T(8,128)(2,1)S(1)}, u32[]{:S(2)}) copy-start(bf16[128,1024]{1,0:T(8,128)(2,1)S(1)} %collective-permute-done.6.refs_5_) | copy-start | bytes 786436
  120.3 14.6 %collective-permute-start.14 = (bf16[128,512]{1,0:T(8,128)(2,1)}, bf16[128,512]{1,0:T(8,128)(2,1)S(1)}, u32[]{:S(2)}, u32[]{:S(2)}) collective-permute-start(bf16[128,512]{1,0:T(8,128)(2,1)} %attend.8.refs_12_), channel_id=1, source_target_pairs={{0,1},{1,2},{2,3},{3,0},{4,5},{5,6},{6,7},{7,4},{8,9},{9,10},{10,1... | collective-permute-start | bytes 393224 | tf_op jit(solution)/shard_map/ppermute | solution.py:35
  121.8 14.3 %collective-permute-start.13 = (bf16[128,512]{1,0:T(8,128)(2,1)}, bf16[128,512]{1,0:T(8,128)(2,1)S(1)}, u32[]{:S(2)}, u32[]{:S(2)}) collective-permute-start(bf16[128,512]{1,0:T(8,128)(2,1)} %attend.8.refs_12_), channel_id=1, source_target_pairs={{0,2},{1,3},{2,0},{3,1},{4,6},{5,7},{6,4},{7,5},{8,10},{9,11},{10,... | collective-permute-start | bytes 393224 | tf_op jit(solution)/shard_map/ppermute | solution.py:35
  121.9 11.0 %copy-start.8 = (bf16[128,1024]{1,0:T(8,128)(2,1)}, bf16[128,1024]{1,0:T(8,128)(2,1)S(1)}, u32[]{:S(2)}) copy-start(bf16[128,1024]{1,0:T(8,128)(2,1)S(1)} %collective-permute-done.11.refs_11_) | copy-start | bytes 786436
  121.9 14.2 %collective-permute-start.12 = (bf16[128,512]{1,0:T(8,128)(2,1)}, bf16[128,512]{1,0:T(8,128)(2,1)S(1)}, u32[]{:S(2)}, u32[]{:S(2)}) collective-permute-start(bf16[128,512]{1,0:T(8,128)(2,1)} %attend.8.refs_12_), channel_id=1, source_target_pairs={{0,3},{1,0},{2,1},{3,2},{4,7},{5,4},{6,5},{7,6},{8,11},{9,8},{10,9... | collective-permute-start | bytes 393224 | tf_op jit(solution)/shard_map/ppermute | solution.py:35
  124.3 8.5 %copy-start.9 = (bf16[128,1024]{1,0:T(8,128)(2,1)}, bf16[128,1024]{1,0:T(8,128)(2,1)S(1)}, u32[]{:S(2)}) copy-start(bf16[128,1024]{1,0:T(8,128)(2,1)S(1)} %collective-permute-done.10.refs_10_) | copy-start | bytes 786436
  124.3 8.5 %copy-start.10 = (bf16[128,1024]{1,0:T(8,128)(2,1)}, bf16[128,1024]{1,0:T(8,128)(2,1)S(1)}, u32[]{:S(2)}) copy-start(bf16[128,1024]{1,0:T(8,128)(2,1)S(1)} %collective-permute-done.9.refs_9_) | copy-start | bytes 786436
  132.9 6.7 %collective-permute-start.17 = (bf16[128,512]{1,0:T(8,128)(2,1)}, bf16[128,512]{1,0:T(8,128)(2,1)S(1)}, u32[]{:S(2)}, u32[]{:S(2)}) collective-permute-start(bf16[128,512]{1,0:T(8,128)(2,1)} %attend.9.refs_16_), channel_id=1, source_target_pairs={{0,1},{1,2},{2,3},{3,0},{4,5},{5,6},{6,7},{7,4},{8,9},{9,10},{10,1... | collective-permute-start | bytes 393224 | tf_op jit(solution)/shard_map/ppermute | solution.py:35
  133.0 6.6 %collective-permute-start.16 = (bf16[128,512]{1,0:T(8,128)(2,1)}, bf16[128,512]{1,0:T(8,128)(2,1)S(1)}, u32[]{:S(2)}, u32[]{:S(2)}) collective-permute-start(bf16[128,512]{1,0:T(8,128)(2,1)} %attend.9.refs_16_), channel_id=1, source_target_pairs={{0,2},{1,3},{2,0},{3,1},{4,6},{5,7},{6,4},{7,5},{8,10},{9,11},{10,... | collective-permute-start | bytes 393224 | tf_op jit(solution)/shard_map/ppermute | solution.py:35
  134.9 26.5 %copy-start.11 = (bf16[128,512]{1,0:T(8,128)(2,1)}, bf16[128,512]{1,0:T(8,128)(2,1)S(1)}, u32[]{:S(2)}) copy-start(bf16[128,512]{1,0:T(8,128)(2,1)S(1)} %collective-permute-done.14.refs_15_) | copy-start | bytes 393220
  134.9 5.7 %collective-permute-start.15 = (bf16[128,512]{1,0:T(8,128)(2,1)}, bf16[128,512]{1,0:T(8,128)(2,1)S(1)}, u32[]{:S(2)}, u32[]{:S(2)}) collective-permute-start(bf16[128,512]{1,0:T(8,128)(2,1)} %attend.9.refs_16_), channel_id=1, source_target_pairs={{0,3},{1,0},{2,1},{3,2},{4,7},{5,4},{6,5},{7,6},{8,11},{9,8},{10,9... | collective-permute-start | bytes 393224 | tf_op jit(solution)/shard_map/ppermute | solution.py:35
  136.1 25.3 %copy-start.12 = (bf16[128,512]{1,0:T(8,128)(2,1)}, bf16[128,512]{1,0:T(8,128)(2,1)S(1)}, u32[]{:S(2)}) copy-start(bf16[128,512]{1,0:T(8,128)(2,1)S(1)} %collective-permute-done.13.refs_14_) | copy-start | bytes 393220
  136.1 25.3 %copy-start.13 = (bf16[128,512]{1,0:T(8,128)(2,1)}, bf16[128,512]{1,0:T(8,128)(2,1)S(1)}, u32[]{:S(2)}) copy-start(bf16[128,512]{1,0:T(8,128)(2,1)S(1)} %collective-permute-done.12.refs_13_) | copy-start | bytes 393220
  139.6 21.8 %copy-start.14 = (bf16[128,512]{1,0:T(8,128)(2,1)}, bf16[128,512]{1,0:T(8,128)(2,1)S(1)}, u32[]{:S(2)}) copy-start(bf16[128,512]{1,0:T(8,128)(2,1)S(1)} %collective-permute-done.17.refs_19_) | copy-start | bytes 393220
  139.6 21.8 %copy-start.15 = (bf16[128,512]{1,0:T(8,128)(2,1)}, bf16[128,512]{1,0:T(8,128)(2,1)S(1)}, u32[]{:S(2)}) copy-start(bf16[128,512]{1,0:T(8,128)(2,1)S(1)} %collective-permute-done.16.refs_18_) | copy-start | bytes 393220
  140.6 20.8 %copy-start.16 = (bf16[128,512]{1,0:T(8,128)(2,1)}, bf16[128,512]{1,0:T(8,128)(2,1)S(1)}, u32[]{:S(2)}) copy-start(bf16[128,512]{1,0:T(8,128)(2,1)S(1)} %collective-permute-done.15.refs_17_) | copy-start | bytes 393220
  169.5 8.6 %copy-start.17 = (bf16[512,512]{1,0:T(8,128)(2,1)S(1)}, bf16[512,512]{1,0:T(8,128)(2,1)}, u32[]{:S(2)}) copy-start(bf16[512,512]{1,0:T(8,128)(2,1)} %get-tuple-element.28) | copy-start | bytes 1572868
  175.7 15.0 %collective-permute-start.19 = (bf16[512,512]{1,0:T(8,128)(2,1)}, bf16[512,512]{1,0:T(8,128)(2,1)S(1)}, u32[]{:S(2)}, u32[]{:S(2)}) collective-permute-start(bf16[512,512]{1,0:T(8,128)(2,1)} %project_rest.1), channel_id=1, source_target_pairs={{0,4},{4,0},{1,5},{5,1},{2,6},{6,2},{3,7},{7,3},{8,12},{12,8},{9,1... | collective-permute-start | bytes 1572872 | tf_op jit(solution)/shard_map/ppermute | solution.py:35
  178.1 23.8 %collective-permute-start.18 = (bf16[512,512]{1,0:T(8,128)(2,1)S(1)}, bf16[512,512]{1,0:T(8,128)(2,1)S(1)}, u32[]{:S(2)}, u32[]{:S(2)}) collective-permute-start(bf16[512,512]{1,0:T(8,128)(2,1)S(1)} %copy-done.17), channel_id=1, source_target_pairs={{0,4},{4,0},{1,5},{5,1},{2,6},{6,2},{3,7},{7,3},{8,12},{12,8},{9,1... | collective-permute-start | bytes 1572872 | tf_op jit(solution)/shard_map/ppermute | solution.py:35
Sparse Core Ops, SparseCore 0:
  63.5 97.7 all-gather.1

commit v3 on v2

--- a/solution.py
+++ b/solution.py
@@ -167,87 +167,58 @@
     )(own, order, queries, kv)
 
 
-def project_partner(places, order_ref, *refs):
-    pieces, (w_ref, out_ref, all_ref, a_s, sem) = refs[:-5], refs[-5:]
-    n = pl.program_id(0)
-    keep = pltpu.make_async_copy(a_s, all_ref, sem.at[len(pieces)])
-
-    @pl.when(n == 0)
-    def _():
-        run_all(
-            [
-                pltpu.make_async_copy(
-                    piece,
-                    a_s.at[
-                        pl.ds(pl.multiple_of(order_ref[chunk] * BLK, BLK), BLK),
-                        pl.ds(at, piece.shape[1]),
-                    ],
-                    sem.at[i],
-                )
-                for i, (piece, (chunk, at)) in enumerate(zip(pieces, places))
-            ]
-        )
-        keep.start()
-
-    w = w_ref[...].reshape(4096, 256)
-    out = jnp.dot(a_s[...], w, preferred_element_type=jnp.float32)
-    out_ref[...] = out.astype(jnp.bfloat16)
-
-    @pl.when(n == pl.num_programs(0) - 1)
-    def _():
-        keep.wait()
-
-
-def partner_terms(order, pieces, places, weight):
-    return pl.pallas_call(
-        functools.partial(project_partner, places),
-        out_shape=(
-            jax.ShapeDtypeStruct((512, 512), jnp.bfloat16),
-            jax.ShapeDtypeStruct((512, 4096), jnp.bfloat16),
-        ),
-        grid_spec=pltpu.PrefetchScalarGridSpec(
-            num_scalar_prefetch=1,
-            grid=(2,),
-            in_specs=[pl.BlockSpec(memory_space=pl.ANY)] * len(pieces)
-            + [pl.BlockSpec((8, None, None, 512, 256), lambda n, o: (0, 0, 0, 0, n))],
-            out_specs=(
-                pl.BlockSpec((512, 256), lambda n, o: (0, n)),
-                pl.BlockSpec(memory_space=pl.ANY),
-            ),
-            scratch_shapes=[
-                pltpu.VMEM((512, 4096), jnp.bfloat16),
-                pltpu.SemaphoreType.DMA((len(pieces) + 1,)),
-            ],
-        ),
-        compiler_params=pltpu.CompilerParams(vmem_limit_bytes=VMEM_BYTES),
-        cost_estimate=pl.CostEstimate(
-            flops=2 * 512 * 4096 * 512, bytes_accessed=14 << 20, transcendentals=0
-        ),
-        name="project_partner",
-    )(order, *pieces, weight)
-
-
-def project_rest(a_ref, w_ref, out_ref):
+def collect_rows(places, order_ref, *refs):
+    pieces, (rows_ref, sem) = refs[:-2], refs[-2:]
+    run_all(
+        [
+            pltpu.make_async_copy(
+                piece,
+                rows_ref.at[
+                    pl.ds(pl.multiple_of(order_ref[chunk] * BLK, BLK), BLK),
+                    pl.ds(at, piece.shape[1]),
+                ],
+                sem.at[i],
+            )
+            for i, (piece, (chunk, at)) in enumerate(zip(pieces, places))
+        ]
+    )
+
+
+def collected(order, pieces, places):
+    return pl.pallas_call(
+        functools.partial(collect_rows, places),
+        out_shape=jax.ShapeDtypeStruct((512, 4096), jnp.bfloat16),
+        in_specs=[pl.BlockSpec(memory_space=pltpu.SMEM)]
+        + [pl.BlockSpec(memory_space=pl.ANY)] * len(pieces),
+        out_specs=pl.BlockSpec(memory_space=pltpu.VMEM),
+        scratch_shapes=[pltpu.SemaphoreType.DMA((len(pieces),))],
+        compiler_params=pltpu.CompilerParams(vmem_limit_bytes=VMEM_BYTES),
+        cost_estimate=pl.CostEstimate(flops=0, bytes_accessed=8 << 20, transcendentals=0),
+        name="collect_rows",
+    )(order, *pieces)
+
+
+def project_partner(a_ref, w_ref, out_ref):
     w = w_ref[...].reshape(4096, 256)
     out = jnp.dot(a_ref[...], w, preferred_element_type=jnp.float32)
     out_ref[...] = out.astype(jnp.bfloat16)
 
 
-def rest_terms(rows, weight):
-    return pl.pallas_call(
-        project_rest,
-        out_shape=jax.ShapeDtypeStruct((512, 512), jnp.bfloat16),
-        grid=(2,),
+def partner_terms(rows, weight):
+    return pl.pallas_call(
+        project_partner,
+        out_shape=jax.ShapeDtypeStruct((512, 1024), jnp.bfloat16),
+        grid=(4,),
         in_specs=[
             pl.BlockSpec((512, 4096), lambda n: (0, 0)),
-            pl.BlockSpec((8, None, None, 512, 256), lambda n: (0, 1, 0, 0, n)),
+            pl.BlockSpec((8, None, None, 512, 256), lambda n: (0, n // 2, 0, 0, n % 2)),
         ],
         out_specs=pl.BlockSpec((512, 256), lambda n: (0, n)),
         compiler_params=pltpu.CompilerParams(vmem_limit_bytes=VMEM_BYTES),
         cost_estimate=pl.CostEstimate(
-            flops=2 * 512 * 4096 * 512, bytes_accessed=9 << 20, transcendentals=0
+            flops=2 * 512 * 4096 * 1024, bytes_accessed=13 << 20, transcendentals=0
         ),
-        name="project_rest",
+        name="project_partner",
     )(rows, weight)
 
 
@@ -327,12 +298,9 @@
         sets.append([piece] + around)
         places += [(chunk, dz * 1024 + part * 512) for dz in range(4)]
     pieces = [piece for group in sets for piece in group]
-    first_sum, rows = partner_terms(order, pieces, tuple(places), weight)
-    got_first = move(first_sum, ("xh",), lambda a: (a + 1,))
-    second_sum = rest_terms(rows, weight)
-    got_second = move(second_sum, ("xh",), lambda a: (a + 1,))
+    rows = collected(order, pieces, tuple(places))
+    others = move(partner_terms(rows, weight), ("xh",), lambda a: (a + 1,))
     own_sum = own_terms(rows, weight)
-    others = jnp.concatenate([got_first, got_second], axis=1)
     return (own_sum + others.astype(jnp.float32)).astype(jnp.bfloat16)
 
 

time: 214 us -> 210 us (0.981)
  waiting for transfers between devices: 81.7 us -> 70.6 us
  Pallas kernels: 65.4 us -> 75.9 us
  starting transfers between devices: 39.3 us -> 34.2 us
    all_gather x1, waiting for transfers between devices: 20.8 us -> 5.99 us  [per_device(): lax.all_gather(both.reshape(1024, 512), ('y', 'xl', 'c'))]
    pallas_call x5, Pallas kernels: 36.3 us -> 46.9 us  [attention(): pl.pallas_call(functools.partial(attend, chunk, heads), out_shape=jax.Sha...]
    ppermute x20 -> x19, starting transfers between devices: 34.1 us -> 29 us  [move(): return lax.ppermute(block, axes, route)]
    ppermute x20 -> x19, waiting for transfers between devices: 60.8 us -> 64.6 us  [move(): return lax.ppermute(block, axes, route)]
  transfers between devices with their start and end apart: 22 -> 21, of which waited for: 10 -> 8; matrix products, arithmetic and copies ran while one was open for 2% -> 2% of each run, Pallas kernels for 24% -> 32%
where the time goes in v3:
time: 210 us; the launch traced here: 206 us
  Pallas kernels  75.9 us (36%)
  waiting for transfers between devices  70.6 us (34%)
  starting transfers between devices  34.2 us (16%)
  between operations  13.7 us (7%)
  other arithmetic  6.82 us (3%)
  local copies, waits for them, and re-layouts  5.35 us (3%)
    ppermute x19, waiting for transfers between devices, move(): return lax.ppermute(block, axes, route)  64.6 us
    pallas_call x5, Pallas kernels, attention(): pl.pallas_call(functools.partial(attend, chunk, heads), out_shape=jax.Sha...  46.9 us
    ppermute x19, starting transfers between devices, move(): return lax.ppermute(block, axes, route)  29 us
    pallas_call x1, Pallas kernels, own_terms(): pl.pallas_call(project_self, out_shape=jax.ShapeDtypeStruct((512, 1024),...  9.43 us
    pallas_call x1, Pallas kernels, partner_terms(): pl.pallas_call(project_partner, out_shape=jax.ShapeDtypeStruct((512, 1024...  9.18 us
    all_gather x1, waiting for transfers between devices, per_device(): lax.all_gather(both.reshape(1024, 512), ('y', 'xl', 'c'))  5.99 us
    pallas_call x1, Pallas kernels, sorted_kv(): pl.pallas_call(sort_blocks, out_shape=jax.ShapeDtypeStruct((64, 2 * BLK,...  5.39 us
    all_to_all x1, starting transfers between devices, per_device(): mine = lax.all_to_all(copies, ('y', 'xl'), 0, 0, tiled=True)  5.19 us
  transfers between devices with their start and end apart: 21, of which 8 were waited for; matrix products, arithmetic and copies ran while one was open for 2% of the time, Pallas kernels for 32%

profile of v3, /device:TPU:25, one launch (start us, length us, event | category | flops | bytes accessed | tf_op | source)
XLA Modules:
  0.0 206.5 jit_solution(17514977250099387851)
XLA Ops:
  6.5 0.8 slice.9
  7.3 0.1 reshape.36
  7.4 1.0 pad_maximum_fusion.1
  8.5 0.2 pad_maximum_fusion
  8.7 1.6 broadcast_in_dim.38
  10.3 5.2 %all-to-all-start = ((bf16[8,1040,128]{2,1,0:T(8,128)(2,1)}), bf16[8,1040,128]{2,1,0:T(8,128)(2,1)S(1)}, u32[]{:S(2)}, u32[]{:S(2)}) async-start(bf16[8,1040,128]{2,1,0:T(8,128)(2,1)} %broadcast_in_dim.38), calls=%async_computation | async-start | bytes 4259840 | tf_op jit(solution)/shard_map/all_to_all | solution.py:272
  15.5 1.0 constant_dynamic-slice_fusion
  16.6 5.8 %collective-permute-start = (bf16[512,512]{1,0:T(8,128)(2,1)}, bf16[512,512]{1,0:T(8,128)(2,1)S(1)}, u32[]{:S(2)}, u32[]{:S(2)}) collective-permute-start(bf16[512,512]{1,0:T(8,128)(2,1)} %get-tuple-element.28), channel_id=1, source_target_pairs={{0,16},{1,48},{2,80},{3,112},{4,4},{5,36},{6,68},{7,100},{16,113},... | collective-permute-start | bytes 1572872 | tf_op jit(solution)/shard_map/ppermute | solution.py:35
  22.3 2.8 %collective-permute-start.1 = (bf16[512,512]{1,0:T(8,128)(2,1)}, bf16[512,512]{1,0:T(8,128)(2,1)S(1)}, u32[]{:S(2)}, u32[]{:S(2)}) collective-permute-start(bf16[512,512]{1,0:T(8,128)(2,1)} %get-tuple-element.27), channel_id=1, source_target_pairs={{0,0},{1,32},{2,64},{3,96},{4,20},{5,52},{6,84},{7,116},{16,97},{1... | collective-permute-start | bytes 1572872 | tf_op jit(solution)/shard_map/ppermute | solution.py:35
  25.2 37.8 %collective-permute-done = bf16[512,512]{1,0:T(8,128)(2,1)S(1)} collective-permute-done((bf16[512,512]{1,0:T(8,128)(2,1)}, bf16[512,512]{1,0:T(8,128)(2,1)S(1)}, u32[]{:S(2)}, u32[]{:S(2)}) %collective-permute-start) | collective-permute-done | bytes 524320 | tf_op jit(solution)/shard_map/ppermute | solution.py:35
  63.0 0.0 collective-permute-done.1
  63.0 0.0 all-to-all-done.mine_ref
  63.0 1.3 maximum_select_fusion
  64.3 0.0 all-gather.2.cloned.1.call-update
  64.3 2.0 collective-permute-start.2
  66.3 0.2 convert_reduce_fusion
  66.5 0.7 select_reduce_fusion.order_ref
  67.2 0.1 slice_reduce_fusion.1
  67.3 0.1 reshape_squeeze.6
  67.3 2.9 %collective-permute-done.2.other_ref = bf16[8,1040,128]{2,1,0:T(8,128)(2,1)} collective-permute-done((bf16[8,1040,128]{2,1,0:T(8,128)(2,1)S(1)}, bf16[8,1040,128]{2,1,0:T(8,128)(2,1)}, u32[]{:S(2)}, u32[]{:S(2)}) %collective-permute-start.2) | collective-permute-done | bytes 2129952 | tf_op jit(solution)/shard_map/ppermute | solution.py:35
  70.3 0.8 slice_reduce_fusion
  71.1 0.1 reshape_squeeze.7
  71.2 0.6 maximum_convert_fusion.slot_ref
  71.8 5.4 %sort_blocks.1.kv_ref = bf16[64,256,128]{2,1,0:T(8,128)(2,1)} custom-call(s32[64]{0:T(128)} %maximum_convert_fusion.slot_ref, bf16[8,1040,128]{2,1,0:T(8,128)(2,1)} %copy-done, bf16[8,1040,128]{2,1,0:T(8,128)(2,1)} %collective-permute-done.2.other_ref), custom_call_target="tpu_custom_call" | custom-call | bytes 8388608 | tf_op jit(solution)/shard_map/sort_blocks/pallas_call | solution.py:60
  77.2 5.6 %attend.5.refs_0_ = bf16[128,1024]{1,0:T(8,128)(2,1)} custom-call(s32[4]{0:T(128)} %copy-done.17, s32[4]{0:T(128)} %select_reduce_fusion.order_ref, bf16[512,1024]{1,0:T(8,128)(2,1)} %q_ref.5, bf16[64,256,128]{2,1,0:T(8,128)(2,1)} %sort_blocks.1.kv_ref), custom_call_target="tpu_custom_call" | custom-call | flops 10000000000 | bytes 4194304 | tf_op jit(solution)/shard_map/attend/pallas_call | solution.py:141
  82.8 2.0 collective-permute-start.3
  84.8 0.0 collective-permute-start.4
  84.8 0.7 collective-permute-start.5
  85.5 6.4 %attend.6.refs_4_ = bf16[128,1024]{1,0:T(8,128)(2,1)} custom-call(s32[4]{0:T(128)} %copy-done.17, s32[4]{0:T(128)} %select_reduce_fusion.order_ref, bf16[512,1024]{1,0:T(8,128)(2,1)} %q_ref.5, bf16[64,256,128]{2,1,0:T(8,128)(2,1)} %sort_blocks.1.kv_ref), custom_call_target="tpu_custom_call" | custom-call | flops 10000000000 | bytes 4194304 | tf_op jit(solution)/shard_map/attend/pallas_call | solution.py:141
  91.9 2.1 %collective-permute-start.6 = (bf16[128,1024]{1,0:T(8,128)(2,1)}, bf16[128,1024]{1,0:T(8,128)(2,1)S(1)}, u32[]{:S(2)}, u32[]{:S(2)}) collective-permute-start(bf16[128,1024]{1,0:T(8,128)(2,1)} %attend.6.refs_4_), channel_id=1, source_target_pairs={{0,3},{1,0},{2,1},{3,2},{4,7},{5,4},{6,5},{7,6},{8,11},{9,8},{10,9... | collective-permute-start | bytes 786440 | tf_op jit(solution)/shard_map/ppermute | solution.py:35
  94.0 1.7 collective-permute-start.7
  95.7 0.0 collective-permute-done.3.refs_1_
  95.8 0.0 collective-permute-start.8
  95.8 0.0 collective-permute-done.4.refs_2_
  95.8 4.4 %collective-permute-done.5.refs_3_ = bf16[128,1024]{1,0:T(8,128)(2,1)S(1)} collective-permute-done((bf16[128,1024]{1,0:T(8,128)(2,1)}, bf16[128,1024]{1,0:T(8,128)(2,1)S(1)}, u32[]{:S(2)}, u32[]{:S(2)}) %collective-permute-start.5) | collective-permute-done | bytes 262176 | tf_op jit(solution)/shard_map/ppermute | solution.py:35
  100.2 14.8 %attend.7.refs_8_ = bf16[128,1024]{1,0:T(8,128)(2,1)} custom-call(s32[4]{0:T(128)} %copy-done.17, s32[4]{0:T(128)} %select_reduce_fusion.order_ref, bf16[512,1024]{1,0:T(8,128)(2,1)} %q_ref.5, bf16[64,256,128]{2,1,0:T(8,128)(2,1)} %sort_blocks.1.kv_ref), custom_call_target="tpu_custom_call" | custom-call | flops 10000000000 | bytes 4194304 | tf_op jit(solution)/shard_map/attend/pallas_call | solution.py:141
  115.0 0.6 collective-permute-start.10
  115.6 0.0 collective-permute-start.11
  115.6 0.0 collective-permute-done.6.refs_5_
  115.6 2.7 %collective-permute-start.9 = (bf16[128,1024]{1,0:T(8,128)(2,1)}, bf16[128,1024]{1,0:T(8,128)(2,1)S(1)}, u32[]{:S(2)}, u32[]{:S(2)}) collective-permute-start(bf16[128,1024]{1,0:T(8,128)(2,1)} %attend.7.refs_8_), channel_id=1, source_target_pairs={{0,3},{1,0},{2,1},{3,2},{4,7},{5,4},{6,5},{7,6},{8,11},{9,8},{10,9... | collective-permute-start | bytes 786440 | tf_op jit(solution)/shard_map/ppermute | solution.py:35
  118.2 0.0 collective-permute-done.7.refs_6_
  118.2 0.0 collective-permute-done.8.refs_7_
  118.3 10.1 %attend.8.refs_12_ = bf16[128,512]{1,0:T(8,128)(2,1)} custom-call(s32[4]{0:T(128)} %copy-done.17, s32[4]{0:T(128)} %select_reduce_fusion.order_ref, bf16[512,1024]{1,0:T(8,128)(2,1)} %q_ref.5, bf16[64,256,128]{2,1,0:T(8,128)(2,1)} %sort_blocks.1.kv_ref), custom_call_target="tpu_custom_call" | custom-call | flops 5000000000 | bytes 4194304 | tf_op jit(solution)/shard_map/attend/pallas_call | solution.py:141
  128.4 0.3 collective-permute-start.12
  128.7 1.1 collective-permute-start.13
  129.8 0.0 collective-permute-done.10.refs_10_
  129.9 0.8 collective-permute-start.14
  130.6 10.0 %attend.9.refs_16_ = bf16[128,512]{1,0:T(8,128)(2,1)} custom-call(s32[4]{0:T(128)} %copy-done.17, s32[4]{0:T(128)} %select_reduce_fusion.order_ref, bf16[512,1024]{1,0:T(8,128)(2,1)} %q_ref.5, bf16[64,256,128]{2,1,0:T(8,128)(2,1)} %sort_blocks.1.kv_ref), custom_call_target="tpu_custom_call" | custom-call | flops 5000000000 | bytes 4194304 | tf_op jit(solution)/shard_map/attend/pallas_call | solution.py:141
  140.7 2.0 collective-permute-start.15
  142.7 1.1 collective-permute-start.16
  143.8 0.0 collective-permute-done.12.refs_13_
  143.8 0.8 collective-permute-start.17
  144.6 0.0 collective-permute-done.14.refs_15_
  144.6 0.6 collective-permute-done.15.refs_17_
  145.2 3.1 %collective-permute-done.16.refs_18_ = bf16[128,512]{1,0:T(8,128)(2,1)S(1)} collective-permute-done((bf16[128,512]{1,0:T(8,128)(2,1)}, bf16[128,512]{1,0:T(8,128)(2,1)S(1)}, u32[]{:S(2)}, u32[]{:S(2)}) %collective-permute-start.16) | collective-permute-done | bytes 131104 | tf_op jit(solution)/shard_map/ppermute | solution.py:35
  148.3 1.3 collective-permute-done.17.refs_19_
  149.7 0.6 copy-done.16
  150.3 5.0 %collect_rows.1.a_ref = bf16[512,4096]{1,0:T(8,128)(2,1)} custom-call(s32[4]{0:T(128)} %select_reduce_fusion.order_ref, bf16[128,1024]{1,0:T(8,128)(2,1)} %attend.5.refs_0_, bf16[128,1024]{1,0:T(8,128)(2,1)} %copy-done.2, bf16[128,1024]{1,0:T(8,128)(2,1)} %copy-done.3, bf16[128,1024]{1,0:T(8,128)(2,1)} %copy-done.4, bf16[128,1024]{1,0:T(8,128)(2,1)} %attend.6.refs_4_, ...), custom_call_target="tpu_custom_call" | custom-call | bytes 8388608 | tf_op jit(solution)/shard_map/collect_rows/pallas_call | solution.py:188
  155.3 6.0 %all-gather.2.cloned.1.call-done = bf16[16,1024,512]{2,1,0:T(8,128)(2,1)} async-done(((bf16[1,1024,512]{2,1,0:T(8,128)(2,1)}), bf16[16,1024,512]{2,1,0:T(8,128)(2,1)}) %all-gather.2.cloned.1.call-update) | async-done | bytes 16777232 | tf_op jit(solution)/shard_map/all_gather | solution.py:286
  161.3 9.2 %project_partner.1 = bf16[512,1024]{1,0:T(8,128)(2,1)} custom-call(bf16[512,4096]{1,0:T(8,128)(2,1)} %collect_rows.1.a_ref, bf16[8,2,2,512,512]{4,3,2,1,0:T(8,128)(2,1)} %bitcast.7), custom_call_target="tpu_custom_call" | custom-call | flops 4294967296 | bytes 13631488 | tf_op jit(solution)/shard_map/project_partner/pallas_call | solution.py:208
  170.5 2.4 %collective-permute-start.18 = (bf16[512,1024]{1,0:T(8,128)(2,1)}, bf16[512,1024]{1,0:T(8,128)(2,1)S(1)}, u32[]{:S(2)}, u32[]{:S(2)}) collective-permute-start(bf16[512,1024]{1,0:T(8,128)(2,1)} %project_partner.1), channel_id=1, source_target_pairs={{0,4},{4,0},{1,5},{5,1},{2,6},{6,2},{3,7},{7,3},{8,12},{12,8},{9,1... | collective-permute-start | bytes 3145736 | tf_op jit(solution)/shard_map/ppermute | solution.py:35
  172.9 9.4 %project_self.1 = f32[512,1024]{1,0:T(8,128)} custom-call(bf16[512,4096]{1,0:T(8,128)(2,1)} %collect_rows.1.a_ref, bf16[8,2,2,512,512]{4,3,2,1,0:T(8,128)(2,1)} %bitcast.8), custom_call_target="tpu_custom_call" | custom-call | flops 4294967296 | bytes 14680064 | tf_op jit(solution)/shard_map/project_self/pallas_call | solution.py:231
  182.4 14.4 %collective-permute-done.18 = bf16[512,1024]{1,0:T(8,128)(2,1)S(1)} collective-permute-done((bf16[512,1024]{1,0:T(8,128)(2,1)}, bf16[512,1024]{1,0:T(8,128)(2,1)S(1)}, u32[]{:S(2)}, u32[]{:S(2)}) %collective-permute-start.18) | collective-permute-done | bytes 1048608 | tf_op jit(solution)/shard_map/ppermute | solution.py:35
  196.7 2.9 %add_convert_fusion = bf16[512,1024]{1,0:T(8,128)(2,1)} fusion(f32[512,1024]{1,0:T(8,128)} %project_self.1, bf16[512,1024]{1,0:T(8,128)(2,1)S(1)} %collective-permute-done.18), kind=kLoop, calls=%fused_computation | loop fusion | flops 1572864 | bytes 4194304 | tf_op jit(solution)/shard_map/convert_element_type | solution.py:304
  (43 shorter events, 0.1 us)
Async XLA Ops:
  7.3 59.0 %copy-start.17 = (s32[4]{0:T(128)}, s32[4]{0:T(128)S(1)}, u32[]{:S(2)}) copy-start(s32[4]{0:T(128)S(1)} %get-tuple-element.26.own_ref) | copy-start | bytes 52
  10.3 5.2 %copy-start.1 = (bf16[1024,512]{1,0:T(8,128)(2,1)S(1)}, bf16[1024,512]{1,0:T(8,128)(2,1)}, u32[]{:S(2)}) copy-start(bf16[1024,512]{1,0:T(8,128)(2,1)} %param.9) | copy-start | bytes 3145732
  10.3 52.7 %all-to-all-start = ((bf16[8,1040,128]{2,1,0:T(8,128)(2,1)}), bf16[8,1040,128]{2,1,0:T(8,128)(2,1)S(1)}, u32[]{:S(2)}, u32[]{:S(2)}) async-start(bf16[8,1040,128]{2,1,0:T(8,128)(2,1)} %broadcast_in_dim.38), calls=%async_computation | async-start | bytes 4259840 | tf_op jit(solution)/shard_map/all_to_all | solution.py:272
  15.5 145.8 %all-gather.2.cloned.1.call-start = ((), (), s32[]{:S(2)}) async-start(), calls=%async_computation.1 | async-start | bytes 17825792 | tf_op jit(solution)/shard_map/all_gather | solution.py:286
  16.6 46.4 %collective-permute-start = (bf16[512,512]{1,0:T(8,128)(2,1)}, bf16[512,512]{1,0:T(8,128)(2,1)S(1)}, u32[]{:S(2)}, u32[]{:S(2)}) collective-permute-start(bf16[512,512]{1,0:T(8,128)(2,1)} %get-tuple-element.28), channel_id=1, source_target_pairs={{0,16},{1,48},{2,80},{3,112},{4,4},{5,36},{6,68},{7,100},{16,113},... | collective-permute-start | bytes 1572872 | tf_op jit(solution)/shard_map/ppermute | solution.py:35
  22.3 40.6 %collective-permute-start.1 = (bf16[512,512]{1,0:T(8,128)(2,1)}, bf16[512,512]{1,0:T(8,128)(2,1)S(1)}, u32[]{:S(2)}, u32[]{:S(2)}) collective-permute-start(bf16[512,512]{1,0:T(8,128)(2,1)} %get-tuple-element.27), channel_id=1, source_target_pairs={{0,0},{1,32},{2,64},{3,96},{4,20},{5,52},{6,84},{7,116},{16,97},{1... | collective-permute-start | bytes 1572872 | tf_op jit(solution)/shard_map/ppermute | solution.py:35
  63.0 8.8 %copy-start = (bf16[8,1040,128]{2,1,0:T(8,128)(2,1)}, bf16[8,1040,128]{2,1,0:T(8,128)(2,1)S(1)}, u32[]{:S(2)}) copy-start(bf16[8,1040,128]{2,1,0:T(8,128)(2,1)S(1)} %all-to-all-done.mine_ref) | copy-start | bytes 6389764
  64.3 6.0 %collective-permute-start.2 = (bf16[8,1040,128]{2,1,0:T(8,128)(2,1)S(1)}, bf16[8,1040,128]{2,1,0:T(8,128)(2,1)}, u32[]{:S(2)}, u32[]{:S(2)}) collective-permute-start(bf16[8,1040,128]{2,1,0:T(8,128)(2,1)S(1)} %all-to-all-done.mine_ref), channel_id=1, source_target_pairs={{0,8},{8,0},{1,9},{9,1},{2,10},{10,2},{3,11},{11,3},{4,12},{12,4},... | collective-permute-start | bytes 6389768 | tf_op jit(solution)/shard_map/ppermute | solution.py:35
  82.8 13.0 %collective-permute-start.3 = (bf16[128,1024]{1,0:T(8,128)(2,1)}, bf16[128,1024]{1,0:T(8,128)(2,1)S(1)}, u32[]{:S(2)}, u32[]{:S(2)}) collective-permute-start(bf16[128,1024]{1,0:T(8,128)(2,1)} %attend.5.refs_0_), channel_id=1, source_target_pairs={{0,3},{1,0},{2,1},{3,2},{4,7},{5,4},{6,5},{7,6},{8,11},{9,8},{10,9... | collective-permute-start | bytes 786440 | tf_op jit(solution)/shard_map/ppermute | solution.py:35
  84.8 11.0 %collective-permute-start.4 = (bf16[128,1024]{1,0:T(8,128)(2,1)}, bf16[128,1024]{1,0:T(8,128)(2,1)S(1)}, u32[]{:S(2)}, u32[]{:S(2)}) collective-permute-start(bf16[128,1024]{1,0:T(8,128)(2,1)} %attend.5.refs_0_), channel_id=1, source_target_pairs={{0,2},{1,3},{2,0},{3,1},{4,6},{5,7},{6,4},{7,5},{8,10},{9,11},{10,... | collective-permute-start | bytes 786440 | tf_op jit(solution)/shard_map/ppermute | solution.py:35
  84.8 15.3 %collective-permute-start.5 = (bf16[128,1024]{1,0:T(8,128)(2,1)}, bf16[128,1024]{1,0:T(8,128)(2,1)S(1)}, u32[]{:S(2)}, u32[]{:S(2)}) collective-permute-start(bf16[128,1024]{1,0:T(8,128)(2,1)} %attend.5.refs_0_), channel_id=1, source_target_pairs={{0,1},{1,2},{2,3},{3,0},{4,5},{5,6},{6,7},{7,4},{8,9},{9,10},{10,1... | collective-permute-start | bytes 786440 | tf_op jit(solution)/shard_map/ppermute | solution.py:35
  91.9 23.7 %collective-permute-start.6 = (bf16[128,1024]{1,0:T(8,128)(2,1)}, bf16[128,1024]{1,0:T(8,128)(2,1)S(1)}, u32[]{:S(2)}, u32[]{:S(2)}) collective-permute-start(bf16[128,1024]{1,0:T(8,128)(2,1)} %attend.6.refs_4_), channel_id=1, source_target_pairs={{0,3},{1,0},{2,1},{3,2},{4,7},{5,4},{6,5},{7,6},{8,11},{9,8},{10,9... | collective-permute-start | bytes 786440 | tf_op jit(solution)/shard_map/ppermute | solution.py:35
  94.0 24.2 %collective-permute-start.7 = (bf16[128,1024]{1,0:T(8,128)(2,1)}, bf16[128,1024]{1,0:T(8,128)(2,1)S(1)}, u32[]{:S(2)}, u32[]{:S(2)}) collective-permute-start(bf16[128,1024]{1,0:T(8,128)(2,1)} %attend.6.refs_4_), channel_id=1, source_target_pairs={{0,2},{1,3},{2,0},{3,1},{4,6},{5,7},{6,4},{7,5},{8,10},{9,11},{10,... | collective-permute-start | bytes 786440 | tf_op jit(solution)/shard_map/ppermute | solution.py:35
  95.8 19.2 %copy-start.2 = (bf16[128,1024]{1,0:T(8,128)(2,1)}, bf16[128,1024]{1,0:T(8,128)(2,1)S(1)}, u32[]{:S(2)}) copy-start(bf16[128,1024]{1,0:T(8,128)(2,1)S(1)} %collective-permute-done.3.refs_1_) | copy-start | bytes 786436
  95.8 22.5 %collective-permute-start.8 = (bf16[128,1024]{1,0:T(8,128)(2,1)}, bf16[128,1024]{1,0:T(8,128)(2,1)S(1)}, u32[]{:S(2)}, u32[]{:S(2)}) collective-permute-start(bf16[128,1024]{1,0:T(8,128)(2,1)} %attend.6.refs_4_), channel_id=1, source_target_pairs={{0,1},{1,2},{2,3},{3,0},{4,5},{5,6},{6,7},{7,4},{8,9},{9,10},{10,1... | collective-permute-start | bytes 786440 | tf_op jit(solution)/shard_map/ppermute | solution.py:35
  95.8 19.2 %copy-start.3 = (bf16[128,1024]{1,0:T(8,128)(2,1)}, bf16[128,1024]{1,0:T(8,128)(2,1)S(1)}, u32[]{:S(2)}) copy-start(bf16[128,1024]{1,0:T(8,128)(2,1)S(1)} %collective-permute-done.4.refs_2_) | copy-start | bytes 786436
  100.1 14.8 %copy-start.4 = (bf16[128,1024]{1,0:T(8,128)(2,1)}, bf16[128,1024]{1,0:T(8,128)(2,1)S(1)}, u32[]{:S(2)}) copy-start(bf16[128,1024]{1,0:T(8,128)(2,1)S(1)} %collective-permute-done.5.refs_3_) | copy-start | bytes 786436
  115.0 14.9 %collective-permute-start.10 = (bf16[128,1024]{1,0:T(8,128)(2,1)}, bf16[128,1024]{1,0:T(8,128)(2,1)S(1)}, u32[]{:S(2)}, u32[]{:S(2)}) collective-permute-start(bf16[128,1024]{1,0:T(8,128)(2,1)} %attend.7.refs_8_), channel_id=1, source_target_pairs={{0,2},{1,3},{2,0},{3,1},{4,6},{5,7},{6,4},{7,5},{8,10},{9,11},{10,... | collective-permute-start | bytes 786440 | tf_op jit(solution)/shard_map/ppermute | solution.py:35
  115.6 15.1 %collective-permute-start.11 = (bf16[128,1024]{1,0:T(8,128)(2,1)}, bf16[128,1024]{1,0:T(8,128)(2,1)S(1)}, u32[]{:S(2)}, u32[]{:S(2)}) collective-permute-start(bf16[128,1024]{1,0:T(8,128)(2,1)} %attend.7.refs_8_), channel_id=1, source_target_pairs={{0,1},{1,2},{2,3},{3,0},{4,5},{5,6},{6,7},{7,4},{8,9},{9,10},{10,1... | collective-permute-start | bytes 786440 | tf_op jit(solution)/shard_map/ppermute | solution.py:35
  115.6 12.9 %copy-start.5 = (bf16[128,1024]{1,0:T(8,128)(2,1)}, bf16[128,1024]{1,0:T(8,128)(2,1)S(1)}, u32[]{:S(2)}) copy-start(bf16[128,1024]{1,0:T(8,128)(2,1)S(1)} %collective-permute-done.6.refs_5_) | copy-start | bytes 786436
  115.6 15.1 %collective-permute-start.9 = (bf16[128,1024]{1,0:T(8,128)(2,1)}, bf16[128,1024]{1,0:T(8,128)(2,1)S(1)}, u32[]{:S(2)}, u32[]{:S(2)}) collective-permute-start(bf16[128,1024]{1,0:T(8,128)(2,1)} %attend.7.refs_8_), channel_id=1, source_target_pairs={{0,3},{1,0},{2,1},{3,2},{4,7},{5,4},{6,5},{7,6},{8,11},{9,8},{10,9... | collective-permute-start | bytes 786440 | tf_op jit(solution)/shard_map/ppermute | solution.py:35
  118.2 10.2 %copy-start.6 = (bf16[128,1024]{1,0:T(8,128)(2,1)}, bf16[128,1024]{1,0:T(8,128)(2,1)S(1)}, u32[]{:S(2)}) copy-start(bf16[128,1024]{1,0:T(8,128)(2,1)S(1)} %collective-permute-done.7.refs_6_) | copy-start | bytes 786436
  118.2 10.2 %copy-start.7 = (bf16[128,1024]{1,0:T(8,128)(2,1)}, bf16[128,1024]{1,0:T(8,128)(2,1)S(1)}, u32[]{:S(2)}) copy-start(bf16[128,1024]{1,0:T(8,128)(2,1)S(1)} %collective-permute-done.8.refs_7_) | copy-start | bytes 786436
  128.4 15.4 %collective-permute-start.12 = (bf16[128,512]{1,0:T(8,128)(2,1)}, bf16[128,512]{1,0:T(8,128)(2,1)S(1)}, u32[]{:S(2)}, u32[]{:S(2)}) collective-permute-start(bf16[128,512]{1,0:T(8,128)(2,1)} %attend.8.refs_12_), channel_id=1, source_target_pairs={{0,3},{1,0},{2,1},{3,2},{4,7},{5,4},{6,5},{7,6},{8,11},{9,8},{10,9... | collective-permute-start | bytes 393224 | tf_op jit(solution)/shard_map/ppermute | solution.py:35
  128.7 15.9 %collective-permute-start.13 = (bf16[128,512]{1,0:T(8,128)(2,1)}, bf16[128,512]{1,0:T(8,128)(2,1)S(1)}, u32[]{:S(2)}, u32[]{:S(2)}) collective-permute-start(bf16[128,512]{1,0:T(8,128)(2,1)} %attend.8.refs_12_), channel_id=1, source_target_pairs={{0,2},{1,3},{2,0},{3,1},{4,6},{5,7},{6,4},{7,5},{8,10},{9,11},{10,... | collective-permute-start | bytes 393224 | tf_op jit(solution)/shard_map/ppermute | solution.py:35
  129.9 10.8 %copy-start.8 = (bf16[128,1024]{1,0:T(8,128)(2,1)}, bf16[128,1024]{1,0:T(8,128)(2,1)S(1)}, u32[]{:S(2)}) copy-start(bf16[128,1024]{1,0:T(8,128)(2,1)S(1)} %collective-permute-done.10.refs_10_) | copy-start | bytes 786436
  129.9 14.7 %collective-permute-start.14 = (bf16[128,512]{1,0:T(8,128)(2,1)}, bf16[128,512]{1,0:T(8,128)(2,1)S(1)}, u32[]{:S(2)}, u32[]{:S(2)}) collective-permute-start(bf16[128,512]{1,0:T(8,128)(2,1)} %attend.8.refs_12_), channel_id=1, source_target_pairs={{0,1},{1,2},{2,3},{3,0},{4,5},{5,6},{6,7},{7,4},{8,9},{9,10},{10,1... | collective-permute-start | bytes 393224 | tf_op jit(solution)/shard_map/ppermute | solution.py:35
  130.6 10.0 %copy-start.9 = (bf16[128,1024]{1,0:T(8,128)(2,1)}, bf16[128,1024]{1,0:T(8,128)(2,1)S(1)}, u32[]{:S(2)}) copy-start(bf16[128,1024]{1,0:T(8,128)(2,1)S(1)} %collective-permute-done.11.refs_11_) | copy-start | bytes 786436
  130.6 10.0 %copy-start.10 = (bf16[128,1024]{1,0:T(8,128)(2,1)}, bf16[128,1024]{1,0:T(8,128)(2,1)S(1)}, u32[]{:S(2)}) copy-start(bf16[128,1024]{1,0:T(8,128)(2,1)S(1)} %collective-permute-done.9.refs_9_) | copy-start | bytes 786436
  140.7 4.5 %collective-permute-start.15 = (bf16[128,512]{1,0:T(8,128)(2,1)}, bf16[128,512]{1,0:T(8,128)(2,1)S(1)}, u32[]{:S(2)}, u32[]{:S(2)}) collective-permute-start(bf16[128,512]{1,0:T(8,128)(2,1)} %attend.9.refs_16_), channel_id=1, source_target_pairs={{0,3},{1,0},{2,1},{3,2},{4,7},{5,4},{6,5},{7,6},{8,11},{9,8},{10,9... | collective-permute-start | bytes 393224 | tf_op jit(solution)/shard_map/ppermute | solution.py:35
  142.7 5.6 %collective-permute-start.16 = (bf16[128,512]{1,0:T(8,128)(2,1)}, bf16[128,512]{1,0:T(8,128)(2,1)S(1)}, u32[]{:S(2)}, u32[]{:S(2)}) collective-permute-start(bf16[128,512]{1,0:T(8,128)(2,1)} %attend.9.refs_16_), channel_id=1, source_target_pairs={{0,2},{1,3},{2,0},{3,1},{4,6},{5,7},{6,4},{7,5},{8,10},{9,11},{10,... | collective-permute-start | bytes 393224 | tf_op jit(solution)/shard_map/ppermute | solution.py:35
  143.8 5.8 %copy-start.11 = (bf16[128,512]{1,0:T(8,128)(2,1)}, bf16[128,512]{1,0:T(8,128)(2,1)S(1)}, u32[]{:S(2)}) copy-start(bf16[128,512]{1,0:T(8,128)(2,1)S(1)} %collective-permute-done.12.refs_13_) | copy-start | bytes 393220
  143.8 5.8 %collective-permute-start.17 = (bf16[128,512]{1,0:T(8,128)(2,1)}, bf16[128,512]{1,0:T(8,128)(2,1)S(1)}, u32[]{:S(2)}, u32[]{:S(2)}) collective-permute-start(bf16[128,512]{1,0:T(8,128)(2,1)} %attend.9.refs_16_), channel_id=1, source_target_pairs={{0,1},{1,2},{2,3},{3,0},{4,5},{5,6},{6,7},{7,4},{8,9},{9,10},{10,1... | collective-permute-start | bytes 393224 | tf_op jit(solution)/shard_map/ppermute | solution.py:35
  144.6 5.1 %copy-start.12 = (bf16[128,512]{1,0:T(8,128)(2,1)}, bf16[128,512]{1,0:T(8,128)(2,1)S(1)}, u32[]{:S(2)}) copy-start(bf16[128,512]{1,0:T(8,128)(2,1)S(1)} %collective-permute-done.13.refs_14_) | copy-start | bytes 393220
  144.6 5.1 %copy-start.13 = (bf16[128,512]{1,0:T(8,128)(2,1)}, bf16[128,512]{1,0:T(8,128)(2,1)S(1)}, u32[]{:S(2)}) copy-start(bf16[128,512]{1,0:T(8,128)(2,1)S(1)} %collective-permute-done.14.refs_15_) | copy-start | bytes 393220
  145.2 4.5 %copy-start.14 = (bf16[128,512]{1,0:T(8,128)(2,1)}, bf16[128,512]{1,0:T(8,128)(2,1)S(1)}, u32[]{:S(2)}) copy-start(bf16[128,512]{1,0:T(8,128)(2,1)S(1)} %collective-permute-done.15.refs_17_) | copy-start | bytes 393220
  148.3 1.4 copy-start.15
  149.7 0.7 copy-start.16
  170.5 26.2 %collective-permute-start.18 = (bf16[512,1024]{1,0:T(8,128)(2,1)}, bf16[512,1024]{1,0:T(8,128)(2,1)S(1)}, u32[]{:S(2)}, u32[]{:S(2)}) collective-permute-start(bf16[512,1024]{1,0:T(8,128)(2,1)} %project_partner.1), channel_id=1, source_target_pairs={{0,4},{4,0},{1,5},{5,1},{2,6},{6,2},{3,7},{7,3},{8,12},{12,8},{9,1... | collective-permute-start | bytes 3145736 | tf_op jit(solution)/shard_map/ppermute | solution.py:35
Sparse Core Ops, SparseCore 0:
  64.4 96.8 all-gather.1
